TPU v7x, 32 devices: a whole 2x2x4 slice. The times are simulated.
32 devices in a mesh: dp: 4 (over y, x), tensor: 8 (over z, core).
Axes of the slice: x: 2, y: 2, z: 4, core: 2. Of those that a mesh axis runs over, the one named last changes fastest.
Arguments:
- grad_out: bfloat16 [4096, 8192], P('dp', 'tensor'), may hold values from -6 to 6
- acts: bfloat16 [4096, 16384], P('dp', 'tensor'), may hold values from -6 to 6
- weight: bfloat16 [8192, 16384], P('tensor'), may hold values from -0.078125 to 0.078125
- block_mask: int32 [64, 128], replicated, may hold values from 0 to 1, as said below
Outputs:
- grad_acts: bfloat16 [4096, 16384], P('dp', 'tensor')
- grad_weight: float32 [8192, 16384], P(('dp', 'tensor'))
Inputs may be any that keep to these rules, and one draw needn't show every extreme that they name: `block_mask`: kept shares differ between groups of 16 consecutive block columns, from about three twentieths to nine twentieths.
All inputs are finite; a program needn't handle non-finite values.
Results may differ from a plain program's by a relative error of at most 0.001.
Values may be sent and summed in bfloat16 or wider, within the bound.
No kernel may reach another device: no remote copies, remote signals or barrier semaphores. Data moves between devices by JAX's collectives and lax.ppermute only.
A program may use at most 320 MiB of HBM per device.

v0:
```python
import jax
import jax.numpy as jnp
from jax import lax
from jax.sharding import PartitionSpec as P


def expand_mask(mask, side):
    rows, cols = mask.shape
    full = jnp.broadcast_to(mask[:, None, :, None], (rows, side, cols, side))
    return full.reshape(rows * side, cols * side)


def body(grad_out, acts, weight, block_mask):
    group_count = lax.axis_size("dp")
    position = lax.axis_index("tensor")
    d_tile = weight.shape[0]
    full_width = weight.shape[1]
    ff_tile = acts.shape[1]
    side = full_width // block_mask.shape[1]
    row_mask = lax.dynamic_slice_in_dim(block_mask, position * (d_tile // side), d_tile // side, 0)
    kept = weight * expand_mask(row_mask, side).astype(jnp.bfloat16)
    columns = lax.all_to_all(kept, "tensor", split_axis=1, concat_axis=0, tiled=True)
    piece = lax.all_gather(grad_out, "tensor", axis=1, tiled=True)
    input_grad = jnp.dot(piece, columns, preferred_element_type=jnp.float32)
    grad_rows = lax.dot_general(
        piece, acts, (((0,), (0,)), ((), ())), preferred_element_type=jnp.float32
    )
    weight_grad = grad_rows
    input_grad, weight_grad = (input_grad, weight_grad)
    grad_acts = input_grad.astype(jnp.bfloat16)
    col_mask = lax.dynamic_slice_in_dim(
        block_mask, position * (ff_tile // side), ff_tile // side, 1
    )
    scale_factor = 1.0 / (grad_out.shape[0] * group_count) ** 0.5
    weight_grad = weight_grad * expand_mask(col_mask, side).astype(jnp.float32) * scale_factor
    summed = lax.psum_scatter(weight_grad, "dp", scatter_dimension=0, tiled=True)
    grad_weight = lax.all_to_all(summed, "tensor", split_axis=0, concat_axis=1, tiled=True)
    return (grad_acts, grad_weight)


def solution(mesh):
    in_specs = (P("dp", "tensor"), P("dp", "tensor"), P("tensor", None), P())
    out_specs = (P("dp", "tensor"), P(("dp", "tensor"), None))
    return jax.shard_map(body, mesh=mesh, in_specs=in_specs, out_specs=out_specs, check_vma=False)
```

profile of v0, /device:TPU:0, one launch (start us, length us, event | category | flops | bytes accessed | tf_op | source)
XLA Modules:
  0.0 1473.3 jit_solution(16991049544505022486)
XLA Ops:
  7.2 0.0 all-gather.2.cloned.1.call-start
  7.2 0.7 all-gather.2.cloned.1.call-update
  7.9 0.0 reduce-scatter.4.cloned.1.call-start
  7.9 0.8 dynamic-slice_convert_fusion
  8.8 154.6 %all-gather.2.cloned.1.call-done = bf16[1024,8192]{1,0:T(8,128)(2,1)} async-done(((bf16[1024,1024]{1,0:T(8,128)(2,1)}), bf16[1024,8192]{1,0:T(8,128)(2,1)}) %all-gather.2.cloned.1.call-update) | async-done | bytes 16777232 | tf_op jit(solution)/shard_map/all_gather | solution.py:23
  163.4 21.1 %broadcast_in_dim.5 = f32[64,128,16,128]{3,2,1,0:T(8,128)} broadcast(f32[64,16]{1,0:T(8,128)S(1)} %dynamic-slice_convert_fusion), dimensions={0,2} | broadcast | bytes 67112960 | tf_op jit(solution)/shard_map/broadcast_in_dim | solution.py:9
  184.5 75.0 %fusion = f32[8192,2048]{1,0:T(8,128)} fusion(f32[1024,8,16,128]{3,2,1,0:T(8,128)} %bitcast.15, bf16[1024,8192]{1,0:T(8,128)(2,1)} %all-gather.2.cloned.1.call-done, bf16[1024,2048]{1,0:T(8,128)(2,1)} %param.5), kind=kOutput, calls=%fused_computation.1 | convolution fusion | flops 34393292800 | bytes 155189248 | tf_op jit(solution)/shard_map/dot_general | solution.py:25
  259.5 0.0 reduce-scatter.4.cloned.1.call-update
  259.5 0.7 dynamic-slice_convert_fusion.1
  260.2 0.1 copy.15
  260.4 44.2 %copy.16 = bf16[1024,16384]{0,1:T(8,128)(2,1)} copy(bf16[1024,16384]{1,0:T(8,128)(2,1)} %param.6) | data formatting | bytes 67108864 | tf_op args[2]
  304.6 11.7 broadcast_in_dim.4
  316.2 34.7 %bitcast_multiply_fusion.1 = bf16[1024,16384]{0,1:T(8,128)(2,1)} fusion(bf16[1024,16384]{0,1:T(8,128)(2,1)} %copy.16, bf16[2048,8,8,128]{3,2,1,0:T(8,128)(2,1)} %bitcast.26), kind=kLoop, calls=%fused_computation.2 | loop fusion | flops 16777216 | bytes 100663296 | tf_op jit(solution)/shard_map/mul | solution.py:21
  350.9 734.3 %all_to_all.38 = bf16[1024,8,2048]{0,2,1:T(8,128)(2,1)} all-to-all(bf16[1024,8,2048]{0,2,1:T(8,128)(2,1)} %bitcast.27), channel_id=1, replica_groups=mesh['dp'=4,'tensor'=8] {'tensor'}, dimensions={1} | all-to-all | bytes 67108864 | tf_op jit(solution)/shard_map/all_to_all | solution.py:22
  1085.2 0.0 reduce-scatter.4.cloned.1.call-done
  1085.2 5.7 all-to-all-start.1
  1091.0 42.2 %copy.17 = bf16[8,1024,2048]{2,1,0:T(8,128)(2,1)} copy(bf16[8,1024,2048]{1,2,0:T(8,128)(2,1)} %bitcast.28) | data formatting | bytes 67108864 | tf_op jit(solution)/shard_map/all_to_all | solution.py:22
  1133.2 43.3 %convert_bitcast_fusion = bf16[1024,2048]{0,1:T(8,128)(2,1)} fusion(bf16[8192,2048]{1,0:T(8,128)(2,1)} %bitcast.29, bf16[1024,8192]{1,0:T(8,128)(2,1)} %all-gather.2.cloned.1.call-done), kind=kOutput, calls=%fused_computation.3 | convolution fusion | flops 34361835520 | bytes 54525952 | tf_op jit(solution)/shard_map/dot_general | solution.py:24
  1176.5 6.4 copy.19
  1182.9 271.7 %all-to-all-done.1 = f32[8,256,2048]{2,1,0:T(8,128)} async-done(((f32[8,256,2048]{2,1,0:T(8,128)}), f32[8,256,2048]{2,1,0:T(8,128)}, u32[]{:S(2)}, u32[]{:S(2)}) %all-to-all-start.1) | async-done | bytes 16777248 | tf_op jit(solution)/shard_map/all_to_all | solution.py:37
  1454.6 11.8 copy.20
Async XLA Ops:
  7.2 156.3 %all-gather.2.cloned.1.call-start = ((), (), s32[]{:S(2)}) async-start(), calls=%async_computation.3 | async-start | bytes 18874368 | tf_op jit(solution)/shard_map/all_gather | solution.py:23
  7.9 1077.3 %reduce-scatter.4.cloned.1.call-start = ((), (), s32[]{:S(2)}) async-start(), calls=%async_computation.4 | async-start | bytes 83886080
  1085.2 369.4 %all-to-all-start.1 = ((f32[8,256,2048]{2,1,0:T(8,128)}), f32[8,256,2048]{2,1,0:T(8,128)}, u32[]{:S(2)}, u32[]{:S(2)}) async-start(f32[8,256,2048]{2,1,0:T(8,128)} %bitcast.30), calls=%async_computation.1 | async-start | bytes 33554432 | tf_op jit(solution)/shard_map/all_to_all | solution.py:37
Sparse Core Ops, SparseCore 0:
  9.6 153.7 all-gather.1
  259.6 556.3 reduce-scatter.3
where the time goes:
time: 1480 us; the launch traced here: 1470 us
  blocking collectives  734 us (50%)
  waiting for transfers between devices  427 us (29%)
  local copies, waits for them, and re-layouts  138 us (9%)
  matrix products  118 us (8%)
  other arithmetic  36.2 us (2%)
    all_to_all x1, blocking collectives, body(): lax.all_to_all(kept, 'tensor', split_axis=1, concat_axis=0, tiled=True)  734 us
    all_to_all x1, waiting for transfers between devices, body(): lax.all_to_all(summed, 'tensor', split_axis=0, concat_axis=1, tiled=True)  272 us
    all_gather x1, waiting for transfers between devices, body(): piece = lax.all_gather(grad_out, 'tensor', axis=1, tiled=True)  155 us
    dot_general x1, matrix products, body(): lax.dot_general(piece, acts, (((0,), (0,)), ((), ())), preferred_element_...  75 us
    unnamed x2, local copies, waits for them, and re-layouts  50.6 us
    dot_general x1, matrix products, body(): input_grad = jnp.dot(piece, columns, preferred_element_type=jnp.float32)  43.3 us
    all_to_all x1, local copies, waits for them, and re-layouts, body(): lax.all_to_all(kept, 'tensor', split_axis=1, concat_axis=0, tiled=True)  42.2 us
    mul x1, other arithmetic, body(): kept = weight * expand_mask(row_mask, side).astype(jnp.bfloat16)  34.7 us
  transfers between devices with their start and end apart: 3, of which 2 were waited for; matrix products, arithmetic and copies ran while one was open for 13% of the time, Pallas kernels for 0%

commit v1 on v0

v1 whole, which is shorter than its diff:
```python
import jax
import jax.numpy as jnp
from jax import lax
from jax.experimental import pallas as pl
from jax.experimental.pallas import tpu as pltpu
from jax.sharding import PartitionSpec as P

BF16, F32 = jnp.bfloat16, jnp.float32


def ranks(flags):
    n = flags.shape[1]
    before = jnp.arange(n)[:, None] < jnp.arange(n)[None, :]
    return jnp.sum(flags[:, :, None] * before[None], 1)


def slots_to_send(flags, cap, turn):
    n = flags.shape[1]
    wanted = jnp.arange(cap)[None, :, None] + turn * cap
    hit = (ranks(flags)[:, None, :] == wanted) & (flags[:, None, :] > 0)
    return jnp.sum(jnp.where(hit, jnp.arange(n)[None, None, :], 0), 2)


def slots_received(flags, cap, turn):
    slot = ranks(flags) - turn * cap
    return jnp.where((flags > 0) & (slot >= 0) & (slot < cap), slot, -1)


def pack(source, picked, which, shape):
    tiles, cap, height, side, share, ff_tile = shape
    across = ff_tile // side
    by_column = source.shape[1] != ff_tile

    def kernel(which_ref, row_ref, col_ref, in_ref, out_ref):
        base = pl.program_id(0) * cap
        for s in range(cap):
            row = pl.multiple_of(row_ref[base + s], height)
            col = pl.multiple_of(col_ref[base + s], side)
            out_ref[0, s] = in_ref[pl.ds(row, height), pl.ds(col, side)]

    picked = picked.reshape(-1)
    rows, cols = (picked // across) * height, (picked % across) * side
    if by_column:
        place = lambda t, w, r, c: (w[0], t)
    else:
        place = lambda t, w, r, c: (t, 0)
    return pl.pallas_call(
        kernel,
        out_shape=jax.ShapeDtypeStruct((tiles, cap, height, side), source.dtype),
        grid_spec=pltpu.PrefetchScalarGridSpec(
            num_scalar_prefetch=3,
            grid=(tiles,),
            in_specs=[pl.BlockSpec((share, ff_tile), place)],
            out_specs=pl.BlockSpec((1, cap, height, side), lambda t, w, r, c: (t, 0, 0, 0)),
        ),
        cost_estimate=pl.CostEstimate(
            flops=0, transcendentals=0,
            bytes_accessed=2 * tiles * share * ff_tile * source.dtype.itemsize,
        ),
        name="pack",
    )(which.reshape(1).astype(jnp.int32), rows.astype(jnp.int32), cols.astype(jnp.int32), source)


def unpack(blocks, table, share, ff_tile):
    tiles, cap, height, side = blocks.shape
    across = ff_tile // side
    n = table.shape[1]

    def kernel(table_ref, in_ref, out_ref):
        base = pl.program_id(0) * n
        for p in range(n):
            slot = table_ref[base + p]
            value = in_ref[0, jnp.maximum(slot, 0)]
            row, col = (p // across) * height, (p % across) * side
            out_ref[row:row + height, col:col + side] = jnp.where(slot >= 0, value, jnp.zeros_like(value))

    return pl.pallas_call(
        kernel,
        out_shape=jax.ShapeDtypeStruct((share, tiles * ff_tile), blocks.dtype),
        grid_spec=pltpu.PrefetchScalarGridSpec(
            num_scalar_prefetch=1,
            grid=(tiles,),
            in_specs=[pl.BlockSpec((1, cap, height, side), lambda t, s: (t, 0, 0, 0))],
            out_specs=pl.BlockSpec((share, ff_tile), lambda t, s: (0, t)),
        ),
        cost_estimate=pl.CostEstimate(
            flops=0, transcendentals=0, bytes_accessed=8 * tiles * share * ff_tile,
        ),
        name="unpack",
    )(table.reshape(-1).astype(jnp.int32), blocks)


def accumulate(total, features, index, sources, table, share, ff_tile, out_type):
    tiles, tokens = table.shape[0], features.shape[1]
    _, cap, height, side = sources[0][0].shape
    n = table.shape[1]
    across = ff_tile // side
    direct = share % 128 == 0
    cut = tiles // 2
    together = min(cut, max(1, 256 // share))
    depth = together * share
    step = min(tokens, 256)
    steps = cut // together

    def kernel(index_ref, table_ref, *refs):
        lefts, blocks, (total_ref, out_ref, strip, sums) = refs[:2], refs[2:4], refs[4:]

        @pl.when(pl.program_id(0) == 0)
        def _():
            sums[...] = total_ref[...]

        for stream in range(2):
            base = (stream * cut + pl.program_id(0) * together) * n
            for t in range(together):
                for p in range(n):
                    slot = table_ref[base + t * n + p]
                    value = blocks[stream][t, jnp.maximum(slot, 0)]
                    row, col = t * share + (p // across) * height, (p % across) * side
                    strip[stream, row:row + height, col:col + side] = jnp.where(
                        slot >= 0, value, jnp.zeros_like(value)
                    )

        @pl.loop(0, tokens // step)
        def _(m):
            at = pl.ds(pl.multiple_of(m * step, step), step)
            value = sums[at]
            for stream in range(2):
                for t in range(together if direct else 1):
                    size = share if direct else depth
                    value += jnp.dot(
                        lefts[stream][t, at], strip[stream, t * size:(t + 1) * size],
                        preferred_element_type=F32,
                    )
            sums[at] = value

        @pl.when(pl.program_id(0) == steps - 1)
        def _():
            out_ref[...] = sums[...].astype(out_type)

    def left(stream):
        if direct:
            return pl.BlockSpec(
                (together, tokens, share), lambda i, e, s: (stream * steps + i, 0, e[0])
            )
        return pl.BlockSpec((1, tokens, depth), lambda i, e, s: (e[0], 0, stream * steps + i))

    def block(first):
        return pl.BlockSpec(
            (together, cap, height, side), lambda i, e, s: (first // together + i, 0, 0, 0)
        )

    whole = pl.BlockSpec((tokens, ff_tile), lambda i, e, s: (0, 0), pipeline_mode=pl.Buffered(1))
    return pl.pallas_call(
        kernel,
        out_shape=jax.ShapeDtypeStruct((tokens, ff_tile), out_type),
        grid_spec=pltpu.PrefetchScalarGridSpec(
            num_scalar_prefetch=2,
            grid=(steps,),
            in_specs=[left(0), left(1)] + [block(first) for _, first in sources] + [whole],
            out_specs=pl.BlockSpec((tokens, ff_tile), lambda i, e, s: (0, 0)),
            scratch_shapes=[
                pltpu.VMEM((2, depth, ff_tile), BF16), pltpu.VMEM((tokens, ff_tile), F32)
            ],
        ),
        cost_estimate=pl.CostEstimate(
            flops=2 * tokens * tiles * share * ff_tile, transcendentals=0,
            bytes_accessed=2 * tokens * tiles * share + 8 * tokens * ff_tile,
        ),
        name="accumulate",
    )(
        index.reshape(1).astype(jnp.int32), table.reshape(-1).astype(jnp.int32),
        features, features, sources[0][0], sources[1][0], total,
    )


def pairs(count, flip):
    return [(i, i ^ flip) for i in range(count)]


def body(grad_out, acts, weight, block_mask):
    groups = lax.axis_size("dp")
    tiles = lax.axis_size("tensor")
    group = lax.axis_index("dp")
    position = lax.axis_index("tensor")
    tokens, d_tile = grad_out.shape
    ff_tile = acts.shape[1]
    side = weight.shape[1] // block_mask.shape[1]
    share = d_tile // groups
    per = tiles // groups
    rows = per * d_tile
    height = min(side, share)
    down, across = share // height, ff_tile // side
    n = down * across
    cap = -(-3 * n // 4)
    shape = (tiles, cap, height, side, share, ff_tile)

    units = jnp.repeat(block_mask, side // height, axis=0)
    by_weight = units.reshape(tiles, groups, down, tiles, across)
    by_output = units.reshape(groups, tiles, down, tiles, across)
    turns = -(-jnp.maximum(jnp.max(jnp.sum(by_weight, (2, 4))), jnp.max(jnp.sum(by_output, (2, 4)))) // cap)

    def at(array, *where):
        for axis, index in where:
            array = lax.dynamic_index_in_dim(array, index, axis, keepdims=True)
        return array

    weight_out = at(by_weight, (0, position), (1, group))[0, 0].transpose(1, 0, 2).reshape(tiles, n)
    weight_in = at(by_weight, (3, position))[:, :, :, 0].transpose(1, 0, 2, 3).reshape(groups, tiles, n)
    result_out = at(by_output, (0, group), (3, position))[0, :, :, 0].reshape(tiles, n)
    result_in = at(by_output, (0, group), (1, position))[0, 0].transpose(1, 0, 2).reshape(tiles, n)

    def hops(array, flips, axis="dp", count=groups):
        return [lax.ppermute(array(f), axis, pairs(count, f)) for f in flips]

    other_acts = hops(lambda f: acts, (1, 2, 3))
    features = lax.all_gather(grad_out, "tensor", axis=0, tiled=False)

    def packed_weight(turn):
        return pack(weight, slots_to_send(weight_out, cap, turn), group, shape)

    def exchange(array):
        return lax.all_to_all(array, "tensor", split_axis=0, concat_axis=0, tiled=True)

    own, features = lax.optimization_barrier((packed_weight(0), features))
    own = exchange(own)

    core = position % 2
    half = per // 2

    def chosen(flip):
        start = (group ^ flip) * per + core * half
        return lax.dynamic_slice_in_dim(features, start, half, 0)

    got = hops(chosen, (1, 2, 3))
    other = [lax.ppermute(piece, "tensor", pairs(tiles, 1)) for piece in got]
    mine = lax.dynamic_slice_in_dim(features, group * per, per, 0)
    low = [jnp.where(core == 0, a, b) for a, b in zip(got, other)]
    high = [jnp.where(core == 0, b, a) for a, b in zip(got, other)]
    left = jnp.concatenate([mine] + [jnp.concatenate([a, b], 0) for a, b in zip(low, high)], 1)
    right = jnp.concatenate([acts] + other_acts, 0)
    product = jnp.einsum("ptf,th->pfh", left, right, preferred_element_type=F32)
    product = product.reshape(rows, ff_tile)
    scale_factor = 1.0 / (tokens * groups) ** 0.5

    def moved_product(turn):
        blocks = pack(product, slots_to_send(result_out, cap, turn), group, shape)
        blocks = blocks.reshape(tiles, cap * height, side)
        top = jnp.max(jnp.abs(blocks), (1, 2)) * scale_factor
        power = jnp.ceil(jnp.log2(jnp.where(top > 0, top, 1.0)))
        power = jnp.clip(power, -110.0, 110.0) - 12.0
        sent = (blocks * (scale_factor * jnp.exp2(-power))[:, None, None]).astype(jnp.float16)
        note = jnp.broadcast_to(power[:, None, None], (tiles, 16, side)).astype(jnp.float16)
        sent = jnp.concatenate([sent, note], 1)
        got = exchange(sent)
        power = got[:, cap * height, 0].astype(F32)
        blocks = got[:, :cap * height].astype(F32) * jnp.exp2(power)[:, None, None]
        blocks = blocks.reshape(tiles, cap, height, side)
        return unpack(blocks, slots_received(result_in, cap, turn), share, ff_tile)

    grad_weight = moved_product(0)

    if share % 128 == 0:
        lefts = features
    else:
        lefts = features.reshape(tiles, tokens, groups, share).transpose(2, 1, 0, 3)
        lefts = lefts.reshape(groups, tokens, tiles * share)
    cut = tiles // 2

    def add(total, index, sources, turn, out_type=F32):
        table = slots_received(lax.dynamic_index_in_dim(weight_in, index, 0, keepdims=False), cap, turn)
        return accumulate(total, lefts, index, sources, table, share, ff_tile, out_type)

    def more_acts(carry):
        turn, total = carry
        pieces = lax.all_gather(exchange(packed_weight(turn)), "dp", axis=0, tiled=False)

        def one(e, total):
            piece = lax.dynamic_index_in_dim(pieces, e, 0, keepdims=False)
            return add(total, e, ((piece, 0), (piece, cut)), turn)

        return turn + 1, lax.fori_loop(0, groups, one, total)

    def more_weight(carry):
        turn, total = carry
        return turn + 1, total + moved_product(turn)

    def unfinished(carry):
        return carry[0] < turns

    total = jnp.zeros((tokens, ff_tile), F32)
    _, total = lax.while_loop(unfinished, more_acts, (jnp.int32(1), total))
    _, grad_weight = lax.while_loop(unfinished, more_weight, (jnp.int32(1), grad_weight))

    near_x, near_y = hops(lambda f: own, (1, 2))
    far_low = lax.ppermute(near_x[:cut], "dp", pairs(groups, 2))
    far_high = lax.ppermute(near_y[cut:], "dp", pairs(groups, 1))
    total = add(total, group, ((own, 0), (own, cut)), 0)
    total = add(total, group ^ 1, ((near_x, 0), (near_x, cut)), 0)
    total = add(total, group ^ 2, ((near_y, 0), (near_y, cut)), 0)
    total = add(total, group ^ 3, ((far_low, 0), (far_high, 0)), 0, BF16)
    return total, grad_weight


def solution(mesh):
    in_specs = (P("dp", "tensor"), P("dp", "tensor"), P("tensor", None), P())
    out_specs = (P("dp", "tensor"), P(("dp", "tensor"), None))
    return jax.shard_map(body, mesh=mesh, in_specs=in_specs, out_specs=out_specs, check_vma=False)
```

time: 1480 us -> 803 us (0.54)
  blocking collectives: 734 us -> 0 us
  Pallas kernels: 0 us -> 129 us
  local copies, waits for them, and re-layouts: 138 us -> 28.6 us
  waiting for transfers between devices: 427 us -> 502 us
  matrix products: 118 us -> 44.9 us
  starting transfers between devices: 5.81 us -> 23.3 us
    all_to_all x1 -> x0, blocking collectives: 734 us -> none  [body(): lax.all_to_all(kept, 'tensor', split_axis=1, concat_axis=0, tiled=True)]
    ppermute x0 -> x13, waiting for transfers between devices: none -> 363 us  [the longest x8 363 us: hops(): return [lax.ppermute(array(f), axis, pairs(count, f)) for f in flips]]
    all_to_all x1 -> x2, waiting for transfers between devices: 272 us -> 0.01 us  [exchange(): lax.all_to_all(array, 'tensor', split_axis=0, concat_axis=0, tiled=True)]
    pallas_call x0 -> x7, Pallas kernels: none -> 129 us  [the longest x4 92.8 us: accumulate(): pl.pallas_call(kernel, out_shape=jax.ShapeDtypeStruct((tokens, ff_tile),...]
    dot_general x2 -> x1, matrix products: 118 us -> 44.9 us  [body(): product = jnp.einsum('ptf,th->pfh', left, right, preferred_element_type=F32)]
    all_to_all x2 -> x0, local copies, waits for them, and re-layouts: 54 us -> none  [the longest x1 42.2 us: body(): lax.all_to_all(kept, 'tensor', split_axis=1, concat_axis=0, tiled=True)]
    unnamed x2 -> x28, local copies, waits for them, and re-layouts: 50.6 us -> 1.7 us
    broadcast_in_dim x2, local copies, waits for them, and re-layouts: 32.8 us -> 4.32 us  [the longest x1 4.25 us: body(): total = jnp.zeros((tokens, ff_tile), F32)]
  transfers between devices with their start and end apart: 3 -> 16, of which waited for: 2 -> 7; matrix products, arithmetic and copies ran while one was open for 13% -> 15% of each run, Pallas kernels for 0% -> 13%
where the time goes in v1:
time: 803 us; the launch traced here: 794 us
  waiting for transfers between devices  502 us (63%)
  Pallas kernels  129 us (16%)
  other arithmetic  49.5 us (6%)
  matrix products  44.9 us (6%)
  local copies, waits for them, and re-layouts  28.6 us (4%)
  starting transfers between devices  23.3 us (3%)
  between operations  16 us (2%)
    ppermute x8, waiting for transfers between devices, hops(): return [lax.ppermute(array(f), axis, pairs(count, f)) for f in flips]  363 us
    all_gather x1, waiting for transfers between devices, body(): features = lax.all_gather(grad_out, 'tensor', axis=0, tiled=False)  139 us
    pallas_call x4, Pallas kernels, accumulate(): pl.pallas_call(kernel, out_shape=jax.ShapeDtypeStruct((tokens, ff_tile),...  92.8 us
    dot_general x1, matrix products, body(): product = jnp.einsum('ptf,th->pfh', left, right, preferred_element_type=F32)  44.9 us
    pallas_call x2, Pallas kernels, pack(): pl.pallas_call(kernel, out_shape=jax.ShapeDtypeStruct((tiles, cap, height...  23.2 us
  transfers between devices with their start and end apart: 16, of which 7 were waited for; matrix products, arithmetic and copies ran while one was open for 15% of the time, Pallas kernels for 13%

profile of v1, /device:TPU:0, one launch (start us, length us, event | category | flops | bytes accessed | tf_op | source)
XLA Modules:
  0.0 793.9 jit_solution(16662870074961508085)
XLA Ops:
  7.2 0.7 all-gather.8.cloned.1.call-update
  7.9 0.9 reshape_reshape_broadcast_in_dim.7
  8.8 0.9 reshape_reshape_broadcast_in_dim.6
  10.2 1.3 fusion.55
  12.5 0.9 multiply_reduce_fusion.4
  14.3 9.9 %pack.10 = bf16[8,24,128,128]{3,2,1,0:T(8,128)(2,1)} custom-call(s32[1]{0:T(128)} %bitcast.12.which_ref.index_ref, s32[192]{0:T(256)} %get-tuple-element.568.row_ref, s32[192]{0:T(256)} %get-tuple-element.567.col_ref, bf16[1024,16384]{1,0:T(8,128)(2,1)} %in_ref.1), custom_call_target="tpu_custom_call" | custom-call | bytes 16777216 | tf_op jit(solution)/shard_map/pack/pallas_call | solution.py:47
  24.2 139.2 %all-gather.8.cloned.1.call-done = bf16[8192,1024]{1,0:T(8,128)(2,1)} async-done(((bf16[1024,1024]{1,0:T(8,128)(2,1)}), bf16[8192,1024]{1,0:T(8,128)(2,1)}) %all-gather.8.cloned.1.call-update) | async-done | bytes 16777232 | tf_op jit(solution)/shard_map/all_gather | solution.py:216
  163.4 4.9 constant_dynamic-slice_fusion.2
  168.3 2.4 collective-permute-start.8
  171.8 46.1 %collective-permute-done.8 = bf16[1,1024,1024]{2,1,0:T(8,128)(2,1)} collective-permute-done((bf16[1,1024,1024]{2,1,0:T(8,128)(2,1)S(1)}, bf16[1,1024,1024]{2,1,0:T(8,128)(2,1)}, u32[]{:S(2)}, u32[]{:S(2)}) %collective-permute-start.8) | collective-permute-done | bytes 2097184 | tf_op jit(solution)/shard_map/ppermute | solution.py:213
  217.9 2.4 collective-permute-start.12
  220.8 0.6 reduce_sum.194
  221.4 0.6 reduce_sum.195
  222.0 0.6 reduce_max.39
  222.7 0.7 reduce_max.40
  225.1 0.6 fusion.44
  225.7 4.6 constant_dynamic-slice_fusion.3
  230.3 32.5 %collective-permute-done.6 = bf16[1,1024,1024]{2,1,0:T(8,128)(2,1)} collective-permute-done((bf16[1,1024,1024]{2,1,0:T(8,128)(2,1)}, bf16[1,1024,1024]{2,1,0:T(8,128)(2,1)}, u32[]{:S(2)}, u32[]{:S(2)}) %collective-permute-start.6) | collective-permute-done | bytes 2097184 | tf_op jit(solution)/shard_map/ppermute | solution.py:213
  262.9 1.5 collective-permute-start.10
  264.8 4.2 broadcast_in_dim.150
  269.1 4.9 all-to-all-start.2
  274.0 2.5 broadcast_select_fusion.1
  276.5 2.6 broadcast_select_fusion.3
  279.2 2.5 broadcast_select_fusion.5
  281.7 8.5 %fusion.59 = bf16[2,4096,1024]{2,1,0:T(8,128)(2,1)} fusion(bf16[1,1024,1024]{2,1,0:T(8,128)(2,1)S(1)} %get-tuple-element.556, bf16[1,1024,1024]{2,1,0:T(8,128)(2,1)S(1)} %get-tuple-element.555, bf16[1,1024,1024]{2,1,0:T(8,128)(2,1)S(1)} %get-tuple-element.554, bf16[1,1024,1024]{2,1,0:T(8,128)(2,1)S(1)} %get-tuple-element.553, ...), kind=kLoop, calls=%fused_computation.59.clone.2 | loop fusion | flops 117440512 | bytes 33554432 | tf_op jit(solution)/shard_map/ptf,th->pfh/dot_general | solution.py:241
  290.2 62.5 %collective-permute-done.12 = bf16[1024,2048]{1,0:T(8,128)(2,1)} collective-permute-done((bf16[1024,2048]{1,0:T(8,128)(2,1)}, bf16[1024,2048]{1,0:T(8,128)(2,1)}, u32[]{:S(2)}, u32[]{:S(2)}) %collective-permute-start.12) | collective-permute-done | bytes 4194336 | tf_op jit(solution)/shard_map/ppermute | solution.py:213
  352.7 89.1 %collective-permute-done.11 = bf16[1024,2048]{1,0:T(8,128)(2,1)} collective-permute-done((bf16[1024,2048]{1,0:T(8,128)(2,1)}, bf16[1024,2048]{1,0:T(8,128)(2,1)}, u32[]{:S(2)}, u32[]{:S(2)}) %collective-permute-start.11) | collective-permute-done | bytes 4194336 | tf_op jit(solution)/shard_map/ppermute | solution.py:213
  441.9 44.9 %fusion.16 = f32[2,1024,2048]{2,1,0:T(8,128)} fusion(bf16[1024,2048]{1,0:T(8,128)(2,1)} %collective-permute-done.12, bf16[1024,2048]{1,0:T(8,128)(2,1)} %collective-permute-done.11, bf16[1024,2048]{1,0:T(8,128)(2,1)} %collective-permute-done.10, bf16[1024,2048]{1,0:T(8,128)(2,1)} %param.11, bf16[2,4096,1024]{2,1,0:T(8,128)(2,1)} %fusion.59), kind=kOutput, calls=%fused_computation.58 | convolution fusion | flops 34426847232 | bytes 50331648 | tf_op jit(solution)/shard_map/ptf,th->pfh/dot_general | solution.py:241
  486.8 13.3 %pack.11 = f32[8,24,128,128]{3,2,1,0:T(8,128)} custom-call(s32[1]{0:T(128)} %bitcast.12.which_ref.index_ref, s32[192]{0:T(256)} %get-tuple-element.566.row_ref, s32[192]{0:T(256)} %get-tuple-element.565.col_ref, f32[2048,2048]{1,0:T(8,128)} %bitcast.82), custom_call_target="tpu_custom_call" | custom-call | bytes 33554432 | tf_op jit(solution)/shard_map/pack/pallas_call | solution.py:47
  500.1 5.6 abs_reduce_fusion.1
  505.7 6.1 fusion.36
  511.9 4.3 pad_maximum_fusion.1
  516.3 5.0 all-to-all-start.3
  521.3 1.5 collective-permute-start
  522.8 1.0 collective-permute-start.2
  527.2 132.3 %collective-permute-done.refs_2_.refs_3_ = bf16[8,24,128,128]{3,2,1,0:T(8,128)(2,1)} collective-permute-done((bf16[8,24,128,128]{3,2,1,0:T(8,128)(2,1)}, bf16[8,24,128,128]{3,2,1,0:T(8,128)(2,1)}, u32[]{:S(2)}, u32[]{:S(2)}) %collective-permute-start) | collective-permute-done | bytes 6291488 | tf_op jit(solution)/shard_map/ppermute | solution.py:213
  659.5 4.0 slice.30
  663.5 1.4 collective-permute-start.1
  664.9 4.0 slice.31
  668.8 1.1 collective-permute-start.3
  669.9 23.5 %accumulate.11.refs_4_ = f32[1024,2048]{1,0:T(8,128)} custom-call(s32[1]{0:T(128)} %bitcast.12.which_ref.index_ref, s32[256]{0:T(256)} %and_select_fusion.9.table_ref, bf16[8,1024,1024]{2,1,0:T(8,128)(2,1)} %get-tuple-element.933, bf16[8,1024,1024]{2,1,0:T(8,128)(2,1)} %get-tuple-element.933, bf16[8,24,128,128]{3,2,1,0:T(8,128)(2,1)} %all-to-all-done.2.refs_2_.refs_3_, ...), custom_call_target="tpu_custom_call" | custom-call | flops 8589934592 | bytes 20971520 | tf_op jit(solution)/shard_map/accumulate/pallas_call | solution.py:153
  693.4 0.9 fusion.42
  694.3 8.3 %convert_multiply_fusion.1 = f32[8,3072,128]{2,1,0:T(8,128)} fusion(f16[8,3088,128]{2,1,0:T(8,128)(2,1)} %all-to-all-done.3, f32[8]{0:T(128)S(1)} %fusion.42), kind=kLoop, calls=%fused_computation.81 | loop fusion | flops 6291456 | bytes 18874400 | tf_op jit(solution)/shard_map/mul | solution.py:256
  702.5 13.2 %unpack.5 = f32[256,16384]{1,0:T(8,128)} custom-call(s32[256]{0:T(256)} %and_select_fusion.8.table_ref, f32[8,24,128,128]{3,2,1,0:T(8,128)} %bitcast.84), custom_call_target="tpu_custom_call" | custom-call | bytes 33554432 | tf_op jit(solution)/shard_map/unpack/pallas_call | solution.py:77
  715.8 23.5 %accumulate.12.refs_4_ = f32[1024,2048]{1,0:T(8,128)} custom-call(s32[1]{0:T(128)} %bitcast.18.index_ref, s32[256]{0:T(256)} %and_select_fusion.10.table_ref, bf16[8,1024,1024]{2,1,0:T(8,128)(2,1)} %get-tuple-element.933, bf16[8,1024,1024]{2,1,0:T(8,128)(2,1)} %get-tuple-element.933, bf16[8,24,128,128]{3,2,1,0:T(8,128)(2,1)} %collective-permute-done.refs_2_.refs_3_, ...), custom_call_target="tpu_custom_call" | custom-call | flops 8589934592 | bytes 20971520 | tf_op jit(solution)/shard_map/accumulate/pallas_call | solution.py:153
  739.3 23.5 %accumulate.13.refs_4_ = f32[1024,2048]{1,0:T(8,128)} custom-call(s32[1]{0:T(128)} %bitcast.16.index_ref, s32[256]{0:T(256)} %get-tuple-element.571.table_ref, bf16[8,1024,1024]{2,1,0:T(8,128)(2,1)} %get-tuple-element.933, bf16[8,1024,1024]{2,1,0:T(8,128)(2,1)} %get-tuple-element.933, bf16[8,24,128,128]{3,2,1,0:T(8,128)(2,1)} %collective-permute-done.2.refs_2_.refs_3_, ...), custom_call_target="tpu_custom_call" | custom-call | flops 8589934592 | bytes 20971520 | tf_op jit(solution)/shard_map/accumulate/pallas_call | solution.py:153
  762.8 1.6 copy-done.1
  764.4 22.3 %accumulate.14 = bf16[1024,2048]{1,0:T(8,128)(2,1)} custom-call(s32[1]{0:T(128)} %bitcast.8.index_ref, s32[256]{0:T(256)} %get-tuple-element.572.table_ref, bf16[8,1024,1024]{2,1,0:T(8,128)(2,1)} %get-tuple-element.933, bf16[8,1024,1024]{2,1,0:T(8,128)(2,1)} %get-tuple-element.933, bf16[4,24,128,128]{3,2,1,0:T(8,128)(2,1)} %copy-done.1, ...), custom_call_target="tpu_custom_call" | custom-call | flops 8589934592 | bytes 20971520 | tf_op jit(solution)/shard_map/accumulate/pallas_call | solution.py:153
  (88 shorter events, 8.6 us)
Async XLA Ops:
  7.2 156.2 %all-gather.8.cloned.1.call-start = ((), (), s32[]{:S(2)}) async-start(), calls=%async_computation.4 | async-start | bytes 18874368 | tf_op jit(solution)/shard_map/all_gather | solution.py:216
  11.6 213.1 %copy-start.6 = (s32[8,2,16]{2,1,0:T(2,128)}, s32[8,2,16]{2,1,0:T(2,128)S(1)}, u32[]{:S(2)}) copy-start(s32[8,2,16]{2,1,0:T(2,128)S(1)} %copy.88) | copy-start | bytes 3076
  12.4 11.8 %copy-start.4 = (s32[8,2,16]{2,1,0:T(2,128)}, s32[8,2,16]{2,1,0:T(2,128)S(1)}, u32[]{:S(2)}) copy-start(s32[8,2,16]{2,1,0:T(2,128)S(1)} %copy.92) | copy-start | bytes 3076
  12.5 11.7 %copy-start.2 = (s32[8,32]{1,0:T(8,128)}, s32[8,32]{1,0:T(8,128)S(1)}, u32[]{:S(2)}) copy-start(s32[8,32]{1,0:T(8,128)S(1)} %mul.403) | copy-start | bytes 3076
  168.3 49.6 %collective-permute-start.8 = (bf16[1,1024,1024]{2,1,0:T(8,128)(2,1)S(1)}, bf16[1,1024,1024]{2,1,0:T(8,128)(2,1)}, u32[]{:S(2)}, u32[]{:S(2)}) collective-permute-start(bf16[1,1024,1024]{2,1,0:T(8,128)(2,1)S(1)} %get-tuple-element.549), channel_id=1, source_target_pairs={{0,24},{8,16},{16,8},{24,0},{1,25},{9,17},{17,9},{25,1},{2,26},{10... | collective-permute-start | bytes 6291464 | tf_op jit(solution)/shard_map/ppermute | solution.py:213
  170.7 92.2 %collective-permute-start.6 = (bf16[1,1024,1024]{2,1,0:T(8,128)(2,1)}, bf16[1,1024,1024]{2,1,0:T(8,128)(2,1)}, u32[]{:S(2)}, u32[]{:S(2)}) collective-permute-start(bf16[1,1024,1024]{2,1,0:T(8,128)(2,1)} %get-tuple-element.550), channel_id=1, source_target_pairs={{0,16},{8,24},{16,0},{24,8},{1,17},{9,25},{17,1},{25,9},{2,18},{10... | collective-permute-start | bytes 6291464 | tf_op jit(solution)/shard_map/ppermute | solution.py:213
  171.2 93.1 %collective-permute-start.4 = (bf16[1,1024,1024]{2,1,0:T(8,128)(2,1)S(1)}, bf16[1,1024,1024]{2,1,0:T(8,128)(2,1)}, u32[]{:S(2)}, u32[]{:S(2)}) collective-permute-start(bf16[1,1024,1024]{2,1,0:T(8,128)(2,1)S(1)} %get-tuple-element.548), channel_id=1, source_target_pairs={{0,8},{8,0},{16,24},{24,16},{1,9},{9,1},{17,25},{25,17},{2,10},{10... | collective-permute-start | bytes 6291464 | tf_op jit(solution)/shard_map/ppermute | solution.py:213
  217.8 46.5 %collective-permute-start.9 = (bf16[1,1024,1024]{2,1,0:T(8,128)(2,1)}, bf16[1,1024,1024]{2,1,0:T(8,128)(2,1)}, u32[]{:S(2)}, u32[]{:S(2)}) collective-permute-start(bf16[1,1024,1024]{2,1,0:T(8,128)(2,1)} %collective-permute-done.8), channel_id=1, source_target_pairs={{0,1},{1,0},{2,3},{3,2},{4,5},{5,4},{6,7},{7,6},{8,9},{9,8},{10,11... | collective-permute-start | bytes 6291464 | tf_op jit(solution)/shard_map/ppermute | solution.py:235
  217.9 134.9 %collective-permute-start.12 = (bf16[1024,2048]{1,0:T(8,128)(2,1)}, bf16[1024,2048]{1,0:T(8,128)(2,1)}, u32[]{:S(2)}, u32[]{:S(2)}) collective-permute-start(bf16[1024,2048]{1,0:T(8,128)(2,1)} %param.11), channel_id=1, source_target_pairs={{0,24},{8,16},{16,8},{24,0},{1,25},{9,17},{17,9},{25,1},{2,26},{10... | collective-permute-start | bytes 12582920 | tf_op jit(solution)/shard_map/ppermute | solution.py:213
  220.2 221.6 %collective-permute-start.11 = (bf16[1024,2048]{1,0:T(8,128)(2,1)}, bf16[1024,2048]{1,0:T(8,128)(2,1)}, u32[]{:S(2)}, u32[]{:S(2)}) collective-permute-start(bf16[1024,2048]{1,0:T(8,128)(2,1)} %param.11), channel_id=1, source_target_pairs={{0,16},{8,24},{16,0},{24,8},{1,17},{9,25},{17,1},{25,9},{2,18},{10... | collective-permute-start | bytes 12582920 | tf_op jit(solution)/shard_map/ppermute | solution.py:213
  262.9 179.0 %collective-permute-start.10 = (bf16[1024,2048]{1,0:T(8,128)(2,1)}, bf16[1024,2048]{1,0:T(8,128)(2,1)}, u32[]{:S(2)}, u32[]{:S(2)}) collective-permute-start(bf16[1024,2048]{1,0:T(8,128)(2,1)} %param.11), channel_id=1, source_target_pairs={{0,8},{8,0},{16,24},{24,16},{1,9},{9,1},{17,25},{25,17},{2,10},{10... | collective-permute-start | bytes 12582920 | tf_op jit(solution)/shard_map/ppermute | solution.py:213
  264.3 12.2 %collective-permute-start.7 = (bf16[1,1024,1024]{2,1,0:T(8,128)(2,1)}, bf16[1,1024,1024]{2,1,0:T(8,128)(2,1)}, u32[]{:S(2)}, u32[]{:S(2)}) collective-permute-start(bf16[1,1024,1024]{2,1,0:T(8,128)(2,1)} %collective-permute-done.6), channel_id=1, source_target_pairs={{0,1},{1,0},{2,3},{3,2},{4,5},{5,4},{6,7},{7,6},{8,9},{9,8},{10,11... | collective-permute-start | bytes 6291464 | tf_op jit(solution)/shard_map/ppermute | solution.py:235
  264.3 14.9 %collective-permute-start.5 = (bf16[1,1024,1024]{2,1,0:T(8,128)(2,1)}, bf16[1,1024,1024]{2,1,0:T(8,128)(2,1)}, u32[]{:S(2)}, u32[]{:S(2)}) collective-permute-start(bf16[1,1024,1024]{2,1,0:T(8,128)(2,1)} %collective-permute-done.4), channel_id=1, source_target_pairs={{0,1},{1,0},{2,3},{3,2},{4,5},{5,4},{6,7},{7,6},{8,9},{9,8},{10,11... | collective-permute-start | bytes 6291464 | tf_op jit(solution)/shard_map/ppermute | solution.py:235
  269.1 247.2 %all-to-all-start.2 = ((bf16[8,24,128,128]{3,2,1,0:T(8,128)(2,1)}), bf16[8,24,128,128]{3,2,1,0:T(8,128)(2,1)}, u32[]{:S(2)}, u32[]{:S(2)}) async-start(bf16[8,24,128,128]{3,2,1,0:T(8,128)(2,1)} %pack.10), calls=%async_computation.2 | async-start | bytes 12582912 | tf_op jit(solution)/shard_map/all_to_all | solution.py:222
  276.5 5.2 copy-start
  516.2 7.6 copy-start.5
  516.2 7.7 copy-start.12
  516.2 7.8 copy-start.11
  516.2 8.0 %copy-start.10 = (s32[8,32]{1,0:T(8,128)S(1)}, s32[8,32]{1,0:T(8,128)}, u32[]{:S(2)}) copy-start(s32[8,32]{1,0:T(8,128)} %get-tuple-element.488) | copy-start | bytes 3076
  516.2 8.2 %copy-start.9 = (s32[8,32]{1,0:T(8,128)S(1)}, s32[8,32]{1,0:T(8,128)}, u32[]{:S(2)}) copy-start(s32[8,32]{1,0:T(8,128)} %get-tuple-element.489) | copy-start | bytes 3076
  516.2 8.3 %copy-start.8 = (s32[8,32]{1,0:T(8,128)S(1)}, s32[8,32]{1,0:T(8,128)}, u32[]{:S(2)}) copy-start(s32[8,32]{1,0:T(8,128)} %get-tuple-element.490) | copy-start | bytes 3076
  516.2 8.4 %copy-start.13 = (pred[8,2,16]{2,0,1:T(8,128)(4,1)S(1)}, pred[8,2,16]{2,0,1:T(8,128)(4,1)}, u32[]{:S(2)}) copy-start(pred[8,2,16]{2,0,1:T(8,128)(4,1)} %get-tuple-element.540) | copy-start | bytes 772
  516.2 8.5 %copy-start.7 = (s32[1,8,2,1,16]{4,3,2,1,0:T(1,128)S(1)}, s32[1,8,2,1,16]{4,3,2,1,0:T(1,128)}, u32[]{:S(2)}) copy-start(s32[1,8,2,1,16]{4,3,2,1,0:T(1,128)} %get-tuple-element.543) | copy-start | bytes 3076
  516.3 177.1 %all-to-all-start.3 = ((f16[8,3088,128]{2,1,0:T(8,128)(2,1)}), f16[8,3088,128]{2,1,0:T(8,128)(2,1)}, u32[]{:S(2)}, u32[]{:S(2)}) async-start(f16[8,3088,128]{2,1,0:T(8,128)(2,1)} %pad_maximum_fusion.1), calls=%async_computation.3 | async-start | bytes 12648448 | tf_op jit(solution)/shard_map/all_to_all | solution.py:222
  521.3 138.2 %collective-permute-start = (bf16[8,24,128,128]{3,2,1,0:T(8,128)(2,1)}, bf16[8,24,128,128]{3,2,1,0:T(8,128)(2,1)}, u32[]{:S(2)}, u32[]{:S(2)}) collective-permute-start(bf16[8,24,128,128]{3,2,1,0:T(8,128)(2,1)} %all-to-all-done.2.refs_2_.refs_3_), channel_id=1, source_target_pairs={{0,8},{8,0},{16,24},{24,16},{1,9},{9,1},{17,25},{25,17},{2,10},{10... | collective-permute-start | bytes 18874376 | tf_op jit(solution)/shard_map/ppermute | solution.py:213
  522.8 142.1 %collective-permute-start.2 = (bf16[8,24,128,128]{3,2,1,0:T(8,128)(2,1)}, bf16[8,24,128,128]{3,2,1,0:T(8,128)(2,1)}, u32[]{:S(2)}, u32[]{:S(2)}) collective-permute-start(bf16[8,24,128,128]{3,2,1,0:T(8,128)(2,1)} %all-to-all-done.2.refs_2_.refs_3_), channel_id=1, source_target_pairs={{0,16},{8,24},{16,0},{24,8},{1,17},{9,25},{17,1},{25,9},{2,18},{10... | collective-permute-start | bytes 18874376 | tf_op jit(solution)/shard_map/ppermute | solution.py:213
  663.5 99.3 %collective-permute-start.1 = (bf16[4,24,128,128]{3,2,1,0:T(8,128)(2,1)}, bf16[4,24,128,128]{3,2,1,0:T(8,128)(2,1)S(1)}, u32[]{:S(2)}, u32[]{:S(2)}) collective-permute-start(bf16[4,24,128,128]{3,2,1,0:T(8,128)(2,1)} %slice.30), channel_id=1, source_target_pairs={{0,16},{8,24},{16,0},{24,8},{1,17},{9,25},{17,1},{25,9},{2,18},{10... | collective-permute-start | bytes 9437192 | tf_op jit(solution)/shard_map/ppermute | solution.py:295
  668.8 93.9 %collective-permute-start.3 = (bf16[4,24,128,128]{3,2,1,0:T(8,128)(2,1)}, bf16[4,24,128,128]{3,2,1,0:T(8,128)(2,1)}, u32[]{:S(2)}, u32[]{:S(2)}) collective-permute-start(bf16[4,24,128,128]{3,2,1,0:T(8,128)(2,1)} %slice.31), channel_id=1, source_target_pairs={{0,8},{8,0},{16,24},{24,16},{1,9},{9,1},{17,25},{25,17},{2,10},{10... | collective-permute-start | bytes 9437192 | tf_op jit(solution)/shard_map/ppermute | solution.py:296
  762.8 1.7 copy-start.1
  764.4 22.3 %copy-start.3 = (s32[8,32]{1,0:T(8,128)S(1)}, s32[8,32]{1,0:T(8,128)}, u32[]{:S(2)}) copy-start(s32[8,32]{1,0:T(8,128)} %copy-done.2) | copy-start | bytes 3076
Sparse Core Ops, SparseCore 0:
  9.6 153.7 all-gather.7

commit v2 on v1

--- a/solution.py
+++ b/solution.py
@@ -14,9 +14,9 @@
     return jnp.sum(flags[:, :, None] * before[None], 1)
 
 
-def slots_to_send(flags, cap, turn):
+def slots_to_send(flags, size, first):
     n = flags.shape[1]
-    wanted = jnp.arange(cap)[None, :, None] + turn * cap
+    wanted = jnp.arange(size)[None, :, None] + first
     hit = (ranks(flags)[:, None, :] == wanted) & (flags[:, None, :] > 0)
     return jnp.sum(jnp.where(hit, jnp.arange(n)[None, None, :], 0), 2)
 
@@ -29,7 +29,6 @@
 def pack(source, picked, which, shape):
     tiles, cap, height, side, share, ff_tile = shape
     across = ff_tile // side
-    by_column = source.shape[1] != ff_tile
 
     def kernel(which_ref, row_ref, col_ref, in_ref, out_ref):
         base = pl.program_id(0) * cap
@@ -40,17 +39,13 @@
 
     picked = picked.reshape(-1)
     rows, cols = (picked // across) * height, (picked % across) * side
-    if by_column:
-        place = lambda t, w, r, c: (w[0], t)
-    else:
-        place = lambda t, w, r, c: (t, 0)
     return pl.pallas_call(
         kernel,
         out_shape=jax.ShapeDtypeStruct((tiles, cap, height, side), source.dtype),
         grid_spec=pltpu.PrefetchScalarGridSpec(
             num_scalar_prefetch=3,
             grid=(tiles,),
-            in_specs=[pl.BlockSpec((share, ff_tile), place)],
+            in_specs=[pl.BlockSpec((share, ff_tile), lambda t, w, r, c: (w[0], t))],
             out_specs=pl.BlockSpec((1, cap, height, side), lambda t, w, r, c: (t, 0, 0, 0)),
         ),
         cost_estimate=pl.CostEstimate(
@@ -59,6 +54,65 @@
         ),
         name="pack",
     )(which.reshape(1).astype(jnp.int32), rows.astype(jnp.int32), cols.astype(jnp.int32), source)
+
+
+def pack_scaled(first, second, picked, core, factor, shape):
+    tiles, cap, height, side, share, ff_tile = shape
+    across = ff_tile // side
+    half = tiles // 2
+
+    def kernel(core_ref, row_ref, col_ref, first_ref, second_ref, out_ref):
+        tile = pl.program_id(0)
+        base = tile * cap
+        swapped = (tile >= half).astype(jnp.int32) != core_ref[0]
+
+        def run(in_ref):
+            def block(s):
+                row = pl.multiple_of(row_ref[base + s], height)
+                col = pl.multiple_of(col_ref[base + s], side)
+                return in_ref[pl.ds(row, height), pl.ds(col, side)]
+
+            top = lax.fori_loop(
+                0, cap, lambda s, top: jnp.maximum(top, jnp.abs(block(s))),
+                jnp.zeros((height, side), F32),
+            )
+            top = jnp.full((16, side), jnp.max(top) * factor, F32)
+            power = jnp.ceil(jnp.log2(jnp.where(top > 0, top, 1.0)))
+            power = jnp.clip(power, -110.0, 110.0) - 12.0
+            scale = jnp.exp2(-power)[:1] * factor
+
+            @pl.loop(0, cap)
+            def _(s):
+                out_ref[0, pl.ds(pl.multiple_of(s * height, height), height)] = block(s) * scale
+
+            out_ref[0, cap * height:] = power
+
+        pl.when(jnp.logical_not(swapped))(lambda: run(first_ref))
+        pl.when(swapped)(lambda: run(second_ref))
+
+    def place(second_half):
+        def index(t, w, r, c):
+            spot = (t + w[0] * half) % tiles
+            return (jnp.clip(spot - half, 0, half - 1) if second_half else jnp.minimum(spot, half - 1), 0)
+
+        return pl.BlockSpec((share, ff_tile), index)
+
+    picked = picked.reshape(-1)
+    rows, cols = (picked // across) * height, (picked % across) * side
+    return pl.pallas_call(
+        kernel,
+        out_shape=jax.ShapeDtypeStruct((tiles, cap * height + 16, side), F32),
+        grid_spec=pltpu.PrefetchScalarGridSpec(
+            num_scalar_prefetch=3,
+            grid=(tiles,),
+            in_specs=[place(False), place(True)],
+            out_specs=pl.BlockSpec((1, cap * height + 16, side), lambda t, w, r, c: (t, 0, 0)),
+        ),
+        cost_estimate=pl.CostEstimate(
+            flops=0, transcendentals=0, bytes_accessed=8 * tiles * share * ff_tile,
+        ),
+        name="pack_scaled",
+    )(core.reshape(1).astype(jnp.int32), rows.astype(jnp.int32), cols.astype(jnp.int32), first, second)
 
 
 def unpack(blocks, table, share, ff_tile):
@@ -92,7 +146,8 @@
 
 def accumulate(total, features, index, sources, table, share, ff_tile, out_type):
     tiles, tokens = table.shape[0], features.shape[1]
-    _, cap, height, side = sources[0][0].shape
+    parts = [part.shape[1] for part in sources[0][0]]
+    height, side = sources[0][0][0].shape[2:]
     n = table.shape[1]
     across = ff_tile // side
     direct = share % 128 == 0
@@ -103,7 +158,17 @@
     steps = cut // together
 
     def kernel(index_ref, table_ref, *refs):
-        lefts, blocks, (total_ref, out_ref, strip, sums) = refs[:2], refs[2:4], refs[4:]
+        lefts, (total_ref, out_ref, strip, sums) = refs[:2], refs[-4:]
+        blocks = refs[2:2 + len(parts)], refs[2 + len(parts):-4]
+
+        def kept(stream, t, slot):
+            value = blocks[stream][0][t, jnp.clip(slot, 0, parts[0] - 1)]
+            before = parts[0]
+            for size, ref in zip(parts[1:], blocks[stream][1:]):
+                later = ref[t, jnp.clip(slot - before, 0, size - 1)]
+                value = jnp.where(slot >= before, later, value)
+                before += size
+            return jnp.where(slot >= 0, value, jnp.zeros_like(value))
 
         @pl.when(pl.program_id(0) == 0)
         def _():
@@ -114,11 +179,8 @@
             for t in range(together):
                 for p in range(n):
                     slot = table_ref[base + t * n + p]
-                    value = blocks[stream][t, jnp.maximum(slot, 0)]
                     row, col = t * share + (p // across) * height, (p % across) * side
-                    strip[stream, row:row + height, col:col + side] = jnp.where(
-                        slot >= 0, value, jnp.zeros_like(value)
-                    )
+                    strip[stream, row:row + height, col:col + side] = kept(stream, t, slot)
 
         @pl.loop(0, tokens // step)
         def _(m):
@@ -144,9 +206,9 @@
             )
         return pl.BlockSpec((1, tokens, depth), lambda i, e, s: (e[0], 0, stream * steps + i))
 
-    def block(first):
+    def block(size, first):
         return pl.BlockSpec(
-            (together, cap, height, side), lambda i, e, s: (first // together + i, 0, 0, 0)
+            (together, size, height, side), lambda i, e, s: (first // together + i, 0, 0, 0)
         )
 
     whole = pl.BlockSpec((tokens, ff_tile), lambda i, e, s: (0, 0), pipeline_mode=pl.Buffered(1))
@@ -156,7 +218,8 @@
         grid_spec=pltpu.PrefetchScalarGridSpec(
             num_scalar_prefetch=2,
             grid=(steps,),
-            in_specs=[left(0), left(1)] + [block(first) for _, first in sources] + [whole],
+            in_specs=[left(0), left(1)]
+            + [block(size, first) for _, first in sources for size in parts] + [whole],
             out_specs=pl.BlockSpec((tokens, ff_tile), lambda i, e, s: (0, 0)),
             scratch_shapes=[
                 pltpu.VMEM((2, depth, ff_tile), BF16), pltpu.VMEM((tokens, ff_tile), F32)
@@ -169,7 +232,7 @@
         name="accumulate",
     )(
         index.reshape(1).astype(jnp.int32), table.reshape(-1).astype(jnp.int32),
-        features, features, sources[0][0], sources[1][0], total,
+        features, features, *sources[0][0], *sources[1][0], total,
     )
 
 
@@ -192,6 +255,7 @@
     down, across = share // height, ff_tile // side
     n = down * across
     cap = -(-3 * n // 4)
+    parts = [cap // 2, cap - cap // 2] if cap > 1 else [cap]
     shape = (tiles, cap, height, side, share, ff_tile)
 
     units = jnp.repeat(block_mask, side // height, axis=0)
@@ -212,45 +276,54 @@
     def hops(array, flips, axis="dp", count=groups):
         return [lax.ppermute(array(f), axis, pairs(count, f)) for f in flips]
 
-    other_acts = hops(lambda f: acts, (1, 2, 3))
+    acts_x, acts_y = hops(lambda f: acts, (1, 2))
+    acts_low = lax.ppermute(acts_x[:tokens // 2], "dp", pairs(groups, 2))
+    acts_high = lax.ppermute(acts_y[tokens // 2:], "dp", pairs(groups, 1))
     features = lax.all_gather(grad_out, "tensor", axis=0, tiled=False)
 
     def packed_weight(turn):
-        return pack(weight, slots_to_send(weight_out, cap, turn), group, shape)
+        made, first = [], turn * cap
+        for size in parts:
+            picked = slots_to_send(weight_out, size, first)
+            made.append(pack(weight, picked, group, (tiles, size) + shape[2:]))
+            first = first + size
+        return made
 
     def exchange(array):
         return lax.all_to_all(array, "tensor", split_axis=0, concat_axis=0, tiled=True)
 
-    own, features = lax.optimization_barrier((packed_weight(0), features))
-    own = exchange(own)
+    own = packed_weight(0)
+    own, features = lax.optimization_barrier((own, features))
+    for i, part in enumerate(own):
+        own[i] = exchange(part)
 
     core = position % 2
     half = per // 2
 
-    def chosen(flip):
-        start = (group ^ flip) * per + core * half
+    def chosen(flip, which=core):
+        start = (group ^ flip) * per + which * half
         return lax.dynamic_slice_in_dim(features, start, half, 0)
 
     got = hops(chosen, (1, 2, 3))
     other = [lax.ppermute(piece, "tensor", pairs(tiles, 1)) for piece in got]
-    mine = lax.dynamic_slice_in_dim(features, group * per, per, 0)
-    low = [jnp.where(core == 0, a, b) for a, b in zip(got, other)]
-    high = [jnp.where(core == 0, b, a) for a, b in zip(got, other)]
-    left = jnp.concatenate([mine] + [jnp.concatenate([a, b], 0) for a, b in zip(low, high)], 1)
-    right = jnp.concatenate([acts] + other_acts, 0)
-    product = jnp.einsum("ptf,th->pfh", left, right, preferred_element_type=F32)
-    product = product.reshape(rows, ff_tile)
+
+    def contract(left, right):
+        out = jnp.einsum("ptf,th->pfh", left, right, preferred_element_type=F32)
+        return out.reshape(rows // 2, ff_tile)
+
+    products = []
+    for pieces in ([chosen(0)] + got, [chosen(0, 1 - core)] + other):
+        product = contract(pieces[0], acts)
+        product = product + contract(pieces[1], acts_x)
+        product = product + contract(pieces[2], acts_y)
+        far = jnp.concatenate([acts_low, acts_high], 0)
+        product = product + contract(pieces[3], far)
+        products.append(product)
     scale_factor = 1.0 / (tokens * groups) ** 0.5
 
     def moved_product(turn):
-        blocks = pack(product, slots_to_send(result_out, cap, turn), group, shape)
-        blocks = blocks.reshape(tiles, cap * height, side)
-        top = jnp.max(jnp.abs(blocks), (1, 2)) * scale_factor
-        power = jnp.ceil(jnp.log2(jnp.where(top > 0, top, 1.0)))
-        power = jnp.clip(power, -110.0, 110.0) - 12.0
-        sent = (blocks * (scale_factor * jnp.exp2(-power))[:, None, None]).astype(jnp.float16)
-        note = jnp.broadcast_to(power[:, None, None], (tiles, 16, side)).astype(jnp.float16)
-        sent = jnp.concatenate([sent, note], 1)
+        picked = slots_to_send(result_out, cap, turn * cap)
+        sent = pack_scaled(*products, picked, core, scale_factor, shape).astype(jnp.float16)
         got = exchange(sent)
         power = got[:, cap * height, 0].astype(F32)
         blocks = got[:, :cap * height].astype(F32) * jnp.exp2(power)[:, None, None]
@@ -272,10 +345,10 @@
 
     def more_acts(carry):
         turn, total = carry
-        pieces = lax.all_gather(exchange(packed_weight(turn)), "dp", axis=0, tiled=False)
+        pieces = [lax.all_gather(exchange(p), "dp", axis=0, tiled=False) for p in packed_weight(turn)]
 
         def one(e, total):
-            piece = lax.dynamic_index_in_dim(pieces, e, 0, keepdims=False)
+            piece = [lax.dynamic_index_in_dim(p, e, 0, keepdims=False) for p in pieces]
             return add(total, e, ((piece, 0), (piece, cut)), turn)
 
         return turn + 1, lax.fori_loop(0, groups, one, total)
@@ -291,9 +364,13 @@
     _, total = lax.while_loop(unfinished, more_acts, (jnp.int32(1), total))
     _, grad_weight = lax.while_loop(unfinished, more_weight, (jnp.int32(1), grad_weight))
 
-    near_x, near_y = hops(lambda f: own, (1, 2))
-    far_low = lax.ppermute(near_x[:cut], "dp", pairs(groups, 2))
-    far_high = lax.ppermute(near_y[cut:], "dp", pairs(groups, 1))
+    near_x, near_y, far_low, far_high = [], [], [], []
+    for part in own:
+        x, y = hops(lambda f: part, (1, 2))
+        far_low.append(lax.ppermute(x[:cut], "dp", pairs(groups, 2)))
+        far_high.append(lax.ppermute(y[cut:], "dp", pairs(groups, 1)))
+        near_x.append(x)
+        near_y.append(y)
     total = add(total, group, ((own, 0), (own, cut)), 0)
     total = add(total, group ^ 1, ((near_x, 0), (near_x, cut)), 0)
     total = add(total, group ^ 2, ((near_y, 0), (near_y, cut)), 0)

time: 803 us -> 642 us (0.80)
  waiting for transfers between devices: 502 us -> 282 us
  matrix products: 44.9 us -> 93.2 us
  other arithmetic: 49.5 us -> 26.6 us
  Pallas kernels: 129 us -> 143 us
  starting transfers between devices: 23.3 us -> 36.3 us
    ppermute x8 -> x9, waiting for transfers between devices: 363 us -> 213 us  [hops(): return [lax.ppermute(array(f), axis, pairs(count, f)) for f in flips]]
    all_gather x1, waiting for transfers between devices: 139 us -> 52.1 us  [body(): features = lax.all_gather(grad_out, 'tensor', axis=0, tiled=False)]
    dot_general x1 -> x8, matrix products: 44.9 us -> 93.2 us  [contract(): out = jnp.einsum('ptf,th->pfh', left, right, preferred_element_type=F32)]
    pallas_call x0 -> x1, Pallas kernels: none -> 16.7 us  [pack_scaled(): pl.pallas_call(kernel, out_shape=jax.ShapeDtypeStruct((tiles, cap * heigh...]
    ppermute x2 -> x6, waiting for transfers between devices: 0.01 us -> 15.8 us  [the longest x2 8.35 us: body(): far_low.append(lax.ppermute(x[:cut], 'dp', pairs(groups, 2)))]
    slice x2 -> x6, local copies, waits for them, and re-layouts: 7.94 us -> 17.2 us  [the longest x2 5.47 us: body(): far_low.append(lax.ppermute(x[:cut], 'dp', pairs(groups, 2)))]
    dot_general x1 -> x0, other arithmetic: 8.52 us -> none  [body(): product = jnp.einsum('ptf,th->pfh', left, right, preferred_element_type=F32)]
  transfers between devices with their start and end apart: 16 -> 22, of which waited for: 7 -> 8; matrix products, arithmetic and copies ran while one was open for 15% -> 23% of each run, Pallas kernels for 13% -> 21%
where the time goes in v2:
time: 642 us; the launch traced here: 633 us
  waiting for transfers between devices  282 us (44%)
  Pallas kernels  143 us (22%)
  matrix products  93.2 us (15%)
  starting transfers between devices  36.3 us (6%)
  local copies, waits for them, and re-layouts  36 us (6%)
  other arithmetic  26.6 us (4%)
  between operations  16.2 us (3%)
    ppermute x9, waiting for transfers between devices, hops(): return [lax.ppermute(array(f), axis, pairs(count, f)) for f in flips]  213 us
    pallas_call x4, Pallas kernels, accumulate(): pl.pallas_call(kernel, out_shape=jax.ShapeDtypeStruct((tokens, ff_tile),...  96.8 us
    dot_general x8, matrix products, contract(): out = jnp.einsum('ptf,th->pfh', left, right, preferred_element_type=F32)  93.2 us
    all_gather x1, waiting for transfers between devices, body(): features = lax.all_gather(grad_out, 'tensor', axis=0, tiled=False)  52.1 us
    pallas_call x1, Pallas kernels, pack_scaled(): pl.pallas_call(kernel, out_shape=jax.ShapeDtypeStruct((tiles, cap * heigh...  16.7 us
    pallas_call x2, Pallas kernels, pack(): pl.pallas_call(kernel, out_shape=jax.ShapeDtypeStruct((tiles, cap, height...  16.5 us
    all_to_all x3, starting transfers between devices, exchange(): lax.all_to_all(array, 'tensor', split_axis=0, concat_axis=0, tiled=True)  14.7 us
    pallas_call x1, Pallas kernels, unpack(): pl.pallas_call(kernel, out_shape=jax.ShapeDtypeStruct((share, tiles * ff_...  13.4 us
  transfers between devices with their start and end apart: 22, of which 8 were waited for; matrix products, arithmetic and copies ran while one was open for 23% of the time, Pallas kernels for 21%

profile of v2, /device:TPU:0, one launch (start us, length us, event | category | flops | bytes accessed | tf_op | source)
XLA Modules:
  0.0 633.4 jit_solution(2551913688142926888)
XLA Ops:
  7.9 3.0 collective-permute-start.9
  10.9 1.5 collective-permute-start.11
  24.0 8.2 %pack.12 = bf16[8,12,128,128]{3,2,1,0:T(8,128)(2,1)} custom-call(s32[1]{0:T(128)} %bitcast.13.which_ref.index_ref, s32[96]{0:T(128)} %get-tuple-element.641.row_ref, s32[96]{0:T(128)} %get-tuple-element.640.col_ref, bf16[1024,16384]{1,0:T(8,128)(2,1)} %in_ref.3), custom_call_target="tpu_custom_call" | custom-call | bytes 16777216 | tf_op jit(solution)/shard_map/pack/pallas_call | solution.py:42
  32.7 8.2 %pack.13 = bf16[8,12,128,128]{3,2,1,0:T(8,128)(2,1)} custom-call(s32[1]{0:T(128)} %bitcast.13.which_ref.index_ref, s32[96]{0:T(128)} %get-tuple-element.639.row_ref, s32[96]{0:T(128)} %get-tuple-element.638.col_ref, bf16[1024,16384]{1,0:T(8,128)(2,1)} %in_ref.3), custom_call_target="tpu_custom_call" | custom-call | bytes 16777216 | tf_op jit(solution)/shard_map/pack/pallas_call | solution.py:42
  41.0 60.9 %collective-permute-done.9 = bf16[1024,2048]{1,0:T(8,128)(2,1)} collective-permute-done((bf16[1024,2048]{1,0:T(8,128)(2,1)}, bf16[1024,2048]{1,0:T(8,128)(2,1)}, u32[]{:S(2)}, u32[]{:S(2)}) %collective-permute-start.9) | collective-permute-done | bytes 4194336 | tf_op jit(solution)/shard_map/ppermute | solution.py:277
  101.8 3.1 slice.50
  104.9 1.8 collective-permute-start.13
  106.7 3.2 slice.51
  109.9 1.5 collective-permute-start.14
  111.4 52.1 %all-gather.13.cloned.1.call-done = bf16[8192,1024]{1,0:T(8,128)(2,1)} async-done(((bf16[1024,1024]{1,0:T(8,128)(2,1)}), bf16[8192,1024]{1,0:T(8,128)(2,1)}) %all-gather.13.cloned.1.call-update) | async-done | bytes 16777232 | tf_op jit(solution)/shard_map/all_gather | solution.py:282
  163.5 4.3 broadcast_in_dim.124
  168.4 3.9 all-to-all-start.3
  173.2 1.8 constant_dynamic-update-slice_fusion.1
  175.1 3.6 constant_dynamic-slice_fusion
  178.7 1.5 collective-permute-start.10
  180.1 1.8 constant_dynamic-update-slice_fusion
  182.0 1.5 collective-permute-start.8
  183.5 8.6 %fusion.27 = f32[1024,2048]{1,0:T(8,128)} fusion(bf16[1024,2048]{1,0:T(8,128)(2,1)S(1)} %copy-done.25, bf16[8,1024,1024]{2,1,0:T(8,128)(2,1)} %get-tuple-element.1050, s32[]{:T(128)S(6)} %select_n.251), kind=kOutput, calls=%fused_computation.71 | convolution fusion | flops 4294967296 | bytes 14680068 | tf_op jit(solution)/shard_map/ptf,th->pfh/dot_general | solution.py:311
  192.2 1.7 collective-permute-start.12
  193.8 8.8 %fusion.17 = f32[1024,2048]{1,0:T(8,128)} fusion(bf16[1024,2048]{1,0:T(8,128)(2,1)S(1)} %copy-done.25, bf16[8,1024,1024]{2,1,0:T(8,128)(2,1)} %get-tuple-element.1050, s32[]{:T(128)S(6)} %select_n.255), kind=kOutput, calls=%fused_computation.63 | convolution fusion | flops 4294967296 | bytes 14680068 | tf_op jit(solution)/shard_map/ptf,th->pfh/dot_general | solution.py:311
  202.7 24.1 %collective-permute-done.10 = bf16[1,1024,1024]{2,1,0:T(8,128)(2,1)} collective-permute-done((bf16[1,1024,1024]{2,1,0:T(8,128)(2,1)S(1)}, bf16[1,1024,1024]{2,1,0:T(8,128)(2,1)}, u32[]{:S(2)}, u32[]{:S(2)}) %collective-permute-start.10) | collective-permute-done | bytes 2097184 | tf_op jit(solution)/shard_map/ppermute | solution.py:277
  226.8 10.8 %fusion.23 = f32[1024,2048]{1,0:T(8,128)} fusion(bf16[1024,2048]{1,0:T(8,128)(2,1)} %collective-permute-done.11, bf16[1,1024,1024]{2,1,0:T(8,128)(2,1)} %collective-permute-done.10), kind=kOutput, calls=%fused_computation.67 | convolution fusion | flops 4294967296 | bytes 14680064 | tf_op jit(solution)/shard_map/ptf,th->pfh/dot_general | solution.py:311
  237.6 10.8 %fusion.25 = f32[1024,2048]{1,0:T(8,128)} fusion(bf16[1024,2048]{1,0:T(8,128)(2,1)} %collective-permute-done.9, bf16[1,1024,1024]{2,1,0:T(8,128)(2,1)} %collective-permute-done.8), kind=kOutput, calls=%fused_computation.69 | convolution fusion | flops 4294967296 | bytes 14680064 | tf_op jit(solution)/shard_map/ptf,th->pfh/dot_general | solution.py:311
  248.9 26.2 %collective-permute-done.12 = bf16[1,1024,1024]{2,1,0:T(8,128)(2,1)} collective-permute-done((bf16[1,1024,1024]{2,1,0:T(8,128)(2,1)S(1)}, bf16[1,1024,1024]{2,1,0:T(8,128)(2,1)}, u32[]{:S(2)}, u32[]{:S(2)}) %collective-permute-start.12) | collective-permute-done | bytes 2097184 | tf_op jit(solution)/shard_map/ppermute | solution.py:277
  275.0 5.0 all-to-all-start.4
  280.1 18.5 %add_add_fusion.1.first_ref = f32[1024,2048]{1,0:T(8,128)} fusion(f32[1024,2048]{1,0:T(8,128)} %fusion.23, f32[1024,2048]{1,0:T(8,128)} %fusion.27, f32[1024,2048]{1,0:T(8,128)} %fusion.25, bf16[1024,2048]{1,0:T(8,128)(2,1)} %copy-done.7, bf16[1,1024,1024]{2,1,0:T(8,128)(2,1)} %collective-permute-done.12), kind=kOutput, calls=%fused_computation.57 | convolution fusion | flops 4301258752 | bytes 39845888 | tf_op jit(solution)/shard_map/ptf,th->pfh/dot_general | solution.py:311
  298.5 10.8 %fusion.13 = f32[1024,2048]{1,0:T(8,128)} fusion(bf16[1024,2048]{1,0:T(8,128)(2,1)} %collective-permute-done.11, bf16[1,1024,1024]{2,1,0:T(8,128)(2,1)} %collective-permute-done.16), kind=kOutput, calls=%fused_computation.59 | convolution fusion | flops 4294967296 | bytes 14680064 | tf_op jit(solution)/shard_map/ptf,th->pfh/dot_general | solution.py:311
  309.3 11.1 %fusion.15 = f32[1024,2048]{1,0:T(8,128)} fusion(bf16[1024,2048]{1,0:T(8,128)(2,1)} %collective-permute-done.9, bf16[1,1024,1024]{2,1,0:T(8,128)(2,1)} %collective-permute-done.15), kind=kOutput, calls=%fused_computation.61 | convolution fusion | flops 4294967296 | bytes 14680064 | tf_op jit(solution)/shard_map/ptf,th->pfh/dot_general | solution.py:311
  320.5 13.8 %add_add_fusion.second_ref = f32[1024,2048]{1,0:T(8,128)} fusion(f32[1024,2048]{1,0:T(8,128)} %fusion.13, f32[1024,2048]{1,0:T(8,128)} %fusion.17, f32[1024,2048]{1,0:T(8,128)} %fusion.15, bf16[1024,2048]{1,0:T(8,128)(2,1)S(1)} %copy-done.8, bf16[1,1024,1024]{2,1,0:T(8,128)(2,1)} %collective-permute-done.17), kind=kOutput, calls=%fused_computation.56 | convolution fusion | flops 4301258752 | bytes 39845888 | tf_op jit(solution)/shard_map/ptf,th->pfh/dot_general | solution.py:311
  334.3 16.7 %pack_scaled.5 = f32[8,3088,128]{2,1,0:T(8,128)} custom-call(s32[1]{0:T(128)} %bitcast.26.core_ref, s32[192]{0:T(256)} %get-tuple-element.637.row_ref, s32[192]{0:T(256)} %get-tuple-element.636.col_ref, f32[1024,2048]{1,0:T(8,128)} %add_add_fusion.1.first_ref, f32[1024,2048]{1,0:T(8,128)} %add_add_fusion.second_ref), custom_call_target="tpu_custom_call" | custom-call | bytes 33554432 | tf_op jit(solution)/shard_map/pack_scaled/pallas_call | solution.py:102
  350.9 8.1 %convert_element_type.98 = f16[8,3088,128]{2,1,0:T(8,128)(2,1)} convert(f32[8,3088,128]{2,1,0:T(8,128)} %pack_scaled.5) | non-fusion elementwise | flops 3162112 | bytes 18972672 | tf_op jit(solution)/shard_map/convert_element_type | solution.py:326
  359.1 5.8 all-to-all-start.5
  364.9 1.4 collective-permute-start
  372.2 24.6 %accumulate.11.refs_6_ = f32[1024,2048]{1,0:T(8,128)} custom-call(s32[1]{0:T(128)} %bitcast.13.which_ref.index_ref, s32[256]{0:T(256)} %and_select_fusion.11.table_ref, bf16[8,1024,1024]{2,1,0:T(8,128)(2,1)} %get-tuple-element.1050, bf16[8,1024,1024]{2,1,0:T(8,128)(2,1)} %get-tuple-element.1050, bf16[8,12,128,128]{3,2,1,0:T(8,128)(2,1)} %copy-done, ...), custom_call_target="tpu_custom_call" | custom-call | flops 8589934592 | bytes 20971520 | tf_op jit(solution)/shard_map/accumulate/pallas_call | solution.py:215
  396.8 39.1 %collective-permute-done.refs_2_.refs_4_ = bf16[8,12,128,128]{3,2,1,0:T(8,128)(2,1)} collective-permute-done((bf16[8,12,128,128]{3,2,1,0:T(8,128)(2,1)S(1)}, bf16[8,12,128,128]{3,2,1,0:T(8,128)(2,1)}, u32[]{:S(2)}, u32[]{:S(2)}) %collective-permute-start) | collective-permute-done | bytes 3145760 | tf_op jit(solution)/shard_map/ppermute | solution.py:277
  435.9 2.7 slice.46
  439.9 63.0 %collective-permute-done.2.refs_3_.refs_5_ = bf16[8,12,128,128]{3,2,1,0:T(8,128)(2,1)} collective-permute-done((bf16[8,12,128,128]{3,2,1,0:T(8,128)(2,1)}, bf16[8,12,128,128]{3,2,1,0:T(8,128)(2,1)}, u32[]{:S(2)}, u32[]{:S(2)}) %collective-permute-start.2) | collective-permute-done | bytes 3145760 | tf_op jit(solution)/shard_map/ppermute | solution.py:277
  502.9 2.7 slice.47
  506.9 2.7 slice.48
  509.6 1.4 collective-permute-start.5
  511.1 2.7 slice.49
  514.4 24.5 %accumulate.12.refs_6_ = f32[1024,2048]{1,0:T(8,128)} custom-call(s32[1]{0:T(128)} %bitcast.19.index_ref, s32[256]{0:T(256)} %and_select_fusion.12.table_ref, bf16[8,1024,1024]{2,1,0:T(8,128)(2,1)} %get-tuple-element.1050, bf16[8,1024,1024]{2,1,0:T(8,128)(2,1)} %get-tuple-element.1050, bf16[8,12,128,128]{3,2,1,0:T(8,128)(2,1)} %collective-permute-done.refs_2_.refs_4_, ...), custom_call_target="tpu_custom_call" | custom-call | flops 8589934592 | bytes 20971520 | tf_op jit(solution)/shard_map/accumulate/pallas_call | solution.py:215
  538.9 24.6 %accumulate.13.refs_6_ = f32[1024,2048]{1,0:T(8,128)} custom-call(s32[1]{0:T(128)} %bitcast.17.index_ref, s32[256]{0:T(256)} %get-tuple-element.644.table_ref, bf16[8,1024,1024]{2,1,0:T(8,128)(2,1)} %get-tuple-element.1050, bf16[8,1024,1024]{2,1,0:T(8,128)(2,1)} %get-tuple-element.1050, bf16[8,12,128,128]{3,2,1,0:T(8,128)(2,1)} %collective-permute-done.4.refs_2_.refs_4_, ...), custom_call_target="tpu_custom_call" | custom-call | flops 8589934592 | bytes 20971520 | tf_op jit(solution)/shard_map/accumulate/pallas_call | solution.py:215
  563.4 8.4 %collective-permute-done.3.refs_3_ = bf16[4,12,128,128]{3,2,1,0:T(8,128)(2,1)} collective-permute-done((bf16[4,12,128,128]{3,2,1,0:T(8,128)(2,1)}, bf16[4,12,128,128]{3,2,1,0:T(8,128)(2,1)}, u32[]{:S(2)}, u32[]{:S(2)}) %collective-permute-start.3) | collective-permute-done | bytes 1572896 | tf_op jit(solution)/shard_map/ppermute | solution.py:370
  571.8 7.4 %collective-permute-done.7.refs_5_ = bf16[4,12,128,128]{3,2,1,0:T(8,128)(2,1)S(1)} collective-permute-done((bf16[4,12,128,128]{3,2,1,0:T(8,128)(2,1)}, bf16[4,12,128,128]{3,2,1,0:T(8,128)(2,1)S(1)}, u32[]{:S(2)}, u32[]{:S(2)}) %collective-permute-start.7) | collective-permute-done | bytes 1572896 | tf_op jit(solution)/shard_map/ppermute | solution.py:371
  580.4 23.2 %accumulate.14 = bf16[1024,2048]{1,0:T(8,128)(2,1)} custom-call(s32[1]{0:T(128)} %bitcast.9.index_ref, s32[256]{0:T(256)} %get-tuple-element.645.table_ref, bf16[8,1024,1024]{2,1,0:T(8,128)(2,1)} %get-tuple-element.1050, bf16[8,1024,1024]{2,1,0:T(8,128)(2,1)} %get-tuple-element.1050, bf16[4,12,128,128]{3,2,1,0:T(8,128)(2,1)} %collective-permute-done.1.refs_2_, ...), custom_call_target="tpu_custom_call" | custom-call | flops 8589934592 | bytes 20971520 | tf_op jit(solution)/shard_map/accumulate/pallas_call | solution.py:215
  604.5 8.3 %convert_multiply_fusion.1 = f32[8,3072,128]{2,1,0:T(8,128)} fusion(f16[8,3088,128]{2,1,0:T(8,128)(2,1)} %all-to-all-done.5, f32[8]{0:T(128)S(1)} %fusion.36), kind=kLoop, calls=%fused_computation.55 | loop fusion | flops 6291456 | bytes 18874400 | tf_op jit(solution)/shard_map/mul | solution.py:329
  612.8 13.4 %unpack.5 = f32[256,16384]{1,0:T(8,128)} custom-call(s32[256]{0:T(256)} %and_select_fusion.10.table_ref, f32[8,24,128,128]{3,2,1,0:T(8,128)} %bitcast.103), custom_call_target="tpu_custom_call" | custom-call | bytes 33554432 | tf_op jit(solution)/shard_map/unpack/pallas_call | solution.py:131
  (125 shorter events, 24.5 us)
Async XLA Ops:
  7.2 156.3 %all-gather.13.cloned.1.call-start = ((), (), s32[]{:S(2)}) async-start(), calls=%async_computation.6 | async-start | bytes 18874368 | tf_op jit(solution)/shard_map/all_gather | solution.py:282
  7.9 93.9 %collective-permute-start.9 = (bf16[1024,2048]{1,0:T(8,128)(2,1)}, bf16[1024,2048]{1,0:T(8,128)(2,1)}, u32[]{:S(2)}, u32[]{:S(2)}) collective-permute-start(bf16[1024,2048]{1,0:T(8,128)(2,1)} %param.11), channel_id=1, source_target_pairs={{0,8},{8,0},{16,24},{24,16},{1,9},{9,1},{17,25},{25,17},{2,10},{10... | collective-permute-start | bytes 12582920 | tf_op jit(solution)/shard_map/ppermute | solution.py:277
  10.9 95.8 %collective-permute-start.11 = (bf16[1024,2048]{1,0:T(8,128)(2,1)}, bf16[1024,2048]{1,0:T(8,128)(2,1)}, u32[]{:S(2)}, u32[]{:S(2)}) collective-permute-start(bf16[1024,2048]{1,0:T(8,128)(2,1)} %param.11), channel_id=1, source_target_pairs={{0,16},{8,24},{16,0},{24,8},{1,17},{9,25},{17,1},{25,9},{2,18},{10... | collective-permute-start | bytes 12582920 | tf_op jit(solution)/shard_map/ppermute | solution.py:277
  18.1 14.1 %copy-start.15 = (s32[8,2,16]{2,1,0:T(2,128)}, s32[8,2,16]{2,1,0:T(2,128)S(1)}, u32[]{:S(2)}) copy-start(s32[8,2,16]{2,1,0:T(2,128)S(1)} %copy.74) | copy-start | bytes 3076
  20.9 11.3 %copy-start.13 = (s32[8,2,16]{2,1,0:T(2,128)}, s32[8,2,16]{2,1,0:T(2,128)S(1)}, u32[]{:S(2)}) copy-start(s32[8,2,16]{2,1,0:T(2,128)S(1)} %copy.80) | copy-start | bytes 3076
  21.0 11.2 %copy-start.11 = (s32[8,32]{1,0:T(8,128)}, s32[8,32]{1,0:T(8,128)S(1)}, u32[]{:S(2)}) copy-start(s32[8,32]{1,0:T(8,128)S(1)} %mul.371) | copy-start | bytes 3076
  104.9 68.3 %collective-permute-start.13 = (bf16[512,2048]{1,0:T(8,128)(2,1)}, bf16[512,2048]{1,0:T(8,128)(2,1)}, u32[]{:S(2)}, u32[]{:S(2)}) collective-permute-start(bf16[512,2048]{1,0:T(8,128)(2,1)} %slice.50), channel_id=1, source_target_pairs={{0,16},{8,24},{16,0},{24,8},{1,17},{9,25},{17,1},{25,9},{2,18},{10... | collective-permute-start | bytes 6291464 | tf_op jit(solution)/shard_map/ppermute | solution.py:280
  109.9 70.3 %collective-permute-start.14 = (bf16[512,2048]{1,0:T(8,128)(2,1)}, bf16[512,2048]{1,0:T(8,128)(2,1)}, u32[]{:S(2)}, u32[]{:S(2)}) collective-permute-start(bf16[512,2048]{1,0:T(8,128)(2,1)} %slice.51), channel_id=1, source_target_pairs={{0,8},{8,0},{16,24},{24,16},{1,9},{9,1},{17,25},{25,17},{2,10},{10... | collective-permute-start | bytes 6291464 | tf_op jit(solution)/shard_map/ppermute | solution.py:281
  167.8 0.6 copy-start.3
  167.8 4.5 copy-start.22
  167.8 4.5 copy-start.24
  168.4 106.6 %all-to-all-start.3 = ((bf16[8,12,128,128]{3,2,1,0:T(8,128)(2,1)}), bf16[8,12,128,128]{3,2,1,0:T(8,128)(2,1)S(1)}, u32[]{:S(2)}, u32[]{:S(2)}) async-start(bf16[8,12,128,128]{3,2,1,0:T(8,128)(2,1)} %pack.12), calls=%async_computation.3 | async-start | bytes 6291456 | tf_op jit(solution)/shard_map/all_to_all | solution.py:293
  178.6 4.9 copy-start.25
  178.7 48.1 %collective-permute-start.10 = (bf16[1,1024,1024]{2,1,0:T(8,128)(2,1)S(1)}, bf16[1,1024,1024]{2,1,0:T(8,128)(2,1)}, u32[]{:S(2)}, u32[]{:S(2)}) collective-permute-start(bf16[1,1024,1024]{2,1,0:T(8,128)(2,1)S(1)} %get-tuple-element.626), channel_id=1, source_target_pairs={{0,16},{8,24},{16,0},{24,8},{1,17},{9,25},{17,1},{25,9},{2,18},{10... | collective-permute-start | bytes 6291464 | tf_op jit(solution)/shard_map/ppermute | solution.py:277
  182.0 10.2 %copy-start.7 = (bf16[1024,2048]{1,0:T(8,128)(2,1)}, bf16[1024,2048]{1,0:T(8,128)(2,1)S(1)}, u32[]{:S(2)}) copy-start(bf16[1024,2048]{1,0:T(8,128)(2,1)S(1)} %constant_dynamic-update-slice_fusion) | copy-start | bytes 12582916
  182.0 55.6 %collective-permute-start.8 = (bf16[1,1024,1024]{2,1,0:T(8,128)(2,1)S(1)}, bf16[1,1024,1024]{2,1,0:T(8,128)(2,1)}, u32[]{:S(2)}, u32[]{:S(2)}) collective-permute-start(bf16[1,1024,1024]{2,1,0:T(8,128)(2,1)S(1)} %get-tuple-element.627), channel_id=1, source_target_pairs={{0,8},{8,0},{16,24},{24,16},{1,9},{9,1},{17,25},{25,17},{2,10},{10... | collective-permute-start | bytes 6291464 | tf_op jit(solution)/shard_map/ppermute | solution.py:277
  192.2 82.9 %collective-permute-start.12 = (bf16[1,1024,1024]{2,1,0:T(8,128)(2,1)S(1)}, bf16[1,1024,1024]{2,1,0:T(8,128)(2,1)}, u32[]{:S(2)}, u32[]{:S(2)}) collective-permute-start(bf16[1,1024,1024]{2,1,0:T(8,128)(2,1)S(1)} %get-tuple-element.625), channel_id=1, source_target_pairs={{0,24},{8,16},{16,8},{24,0},{1,25},{9,17},{17,9},{25,1},{2,26},{10... | collective-permute-start | bytes 6291464 | tf_op jit(solution)/shard_map/ppermute | solution.py:277
  226.8 71.7 %collective-permute-start.16 = (bf16[1,1024,1024]{2,1,0:T(8,128)(2,1)}, bf16[1,1024,1024]{2,1,0:T(8,128)(2,1)}, u32[]{:S(2)}, u32[]{:S(2)}) collective-permute-start(bf16[1,1024,1024]{2,1,0:T(8,128)(2,1)} %collective-permute-done.10), channel_id=1, source_target_pairs={{0,1},{1,0},{2,3},{3,2},{4,5},{5,4},{6,7},{7,6},{8,9},{9,8},{10,11... | collective-permute-start | bytes 6291464 | tf_op jit(solution)/shard_map/ppermute | solution.py:308
  248.4 61.0 %collective-permute-start.15 = (bf16[1,1024,1024]{2,1,0:T(8,128)(2,1)}, bf16[1,1024,1024]{2,1,0:T(8,128)(2,1)}, u32[]{:S(2)}, u32[]{:S(2)}) collective-permute-start(bf16[1,1024,1024]{2,1,0:T(8,128)(2,1)} %collective-permute-done.8), channel_id=1, source_target_pairs={{0,1},{1,0},{2,3},{3,2},{4,5},{5,4},{6,7},{7,6},{8,9},{9,8},{10,11... | collective-permute-start | bytes 6291464 | tf_op jit(solution)/shard_map/ppermute | solution.py:308
  275.0 45.4 %collective-permute-start.17 = (bf16[1,1024,1024]{2,1,0:T(8,128)(2,1)}, bf16[1,1024,1024]{2,1,0:T(8,128)(2,1)}, u32[]{:S(2)}, u32[]{:S(2)}) collective-permute-start(bf16[1,1024,1024]{2,1,0:T(8,128)(2,1)} %collective-permute-done.12), channel_id=1, source_target_pairs={{0,1},{1,0},{2,3},{3,2},{4,5},{5,4},{6,7},{7,6},{8,9},{9,8},{10,11... | collective-permute-start | bytes 6291464 | tf_op jit(solution)/shard_map/ppermute | solution.py:308
  275.0 91.9 %copy-start = (bf16[8,12,128,128]{3,2,1,0:T(8,128)(2,1)}, bf16[8,12,128,128]{3,2,1,0:T(8,128)(2,1)S(1)}, u32[]{:S(2)}) copy-start(bf16[8,12,128,128]{3,2,1,0:T(8,128)(2,1)S(1)} %all-to-all-done.3.refs_2_.refs_4_) | copy-start | bytes 9437188
  275.0 84.0 %all-to-all-start.4 = ((bf16[8,12,128,128]{3,2,1,0:T(8,128)(2,1)}), bf16[8,12,128,128]{3,2,1,0:T(8,128)(2,1)}, u32[]{:S(2)}, u32[]{:S(2)}) async-start(bf16[8,12,128,128]{3,2,1,0:T(8,128)(2,1)} %pack.13), calls=%async_computation.4 | async-start | bytes 6291456 | tf_op jit(solution)/shard_map/all_to_all | solution.py:293
  309.3 11.1 %copy-start.8 = (bf16[1024,2048]{1,0:T(8,128)(2,1)S(1)}, bf16[1024,2048]{1,0:T(8,128)(2,1)}, u32[]{:S(2)}) copy-start(bf16[1024,2048]{1,0:T(8,128)(2,1)} %copy-done.7) | copy-start | bytes 12582916
  359.0 9.9 %copy-start.14 = (s32[8,2,16]{2,1,0:T(2,128)S(1)}, s32[8,2,16]{2,1,0:T(2,128)}, u32[]{:S(2)}) copy-start(s32[8,2,16]{2,1,0:T(2,128)} %copy-done.13) | copy-start | bytes 3076
  359.0 10.0 %copy-start.21 = (s32[8,32]{1,0:T(8,128)S(1)}, s32[8,32]{1,0:T(8,128)}, u32[]{:S(2)}) copy-start(s32[8,32]{1,0:T(8,128)} %get-tuple-element.556) | copy-start | bytes 3076
  359.0 10.1 %copy-start.4 = (s32[4,8,32]{2,1,0:T(8,128)S(1)}, s32[4,8,32]{2,1,0:T(8,128)}, u32[]{:S(2)}) copy-start(s32[4,8,32]{2,1,0:T(8,128)} %copy-done.3) | copy-start | bytes 12292
  359.0 10.2 %copy-start.20 = (s32[8,32]{1,0:T(8,128)S(1)}, s32[8,32]{1,0:T(8,128)}, u32[]{:S(2)}) copy-start(s32[8,32]{1,0:T(8,128)} %get-tuple-element.560) | copy-start | bytes 3076
  359.0 10.3 %copy-start.19 = (s32[8,32]{1,0:T(8,128)S(1)}, s32[8,32]{1,0:T(8,128)}, u32[]{:S(2)}) copy-start(s32[8,32]{1,0:T(8,128)} %get-tuple-element.557) | copy-start | bytes 3076
  359.0 10.5 %copy-start.18 = (s32[8,32]{1,0:T(8,128)S(1)}, s32[8,32]{1,0:T(8,128)}, u32[]{:S(2)}) copy-start(s32[8,32]{1,0:T(8,128)} %get-tuple-element.558) | copy-start | bytes 3076
  359.0 10.7 %copy-start.17 = (s32[8,32]{1,0:T(8,128)S(1)}, s32[8,32]{1,0:T(8,128)}, u32[]{:S(2)}) copy-start(s32[8,32]{1,0:T(8,128)} %get-tuple-element.559) | copy-start | bytes 3076
  359.0 10.7 %copy-start.23 = (pred[8,2,16]{2,0,1:T(8,128)(4,1)S(1)}, pred[8,2,16]{2,0,1:T(8,128)(4,1)}, u32[]{:S(2)}) copy-start(pred[8,2,16]{2,0,1:T(8,128)(4,1)} %get-tuple-element.611) | copy-start | bytes 772
  359.0 10.8 %copy-start.16 = (s32[1,8,2,1,16]{4,3,2,1,0:T(1,128)S(1)}, s32[1,8,2,1,16]{4,3,2,1,0:T(1,128)}, u32[]{:S(2)}) copy-start(s32[1,8,2,1,16]{4,3,2,1,0:T(1,128)} %get-tuple-element.614) | copy-start | bytes 3076
  359.1 244.6 %all-to-all-start.5 = ((f16[8,3088,128]{2,1,0:T(8,128)(2,1)}), f16[8,3088,128]{2,1,0:T(8,128)(2,1)}, u32[]{:S(2)}, u32[]{:S(2)}) async-start(f16[8,3088,128]{2,1,0:T(8,128)(2,1)} %convert_element_type.98), calls=%async_computation.5 | async-start | bytes 12648448 | tf_op jit(solution)/shard_map/all_to_all | solution.py:293
  364.9 71.1 %collective-permute-start = (bf16[8,12,128,128]{3,2,1,0:T(8,128)(2,1)S(1)}, bf16[8,12,128,128]{3,2,1,0:T(8,128)(2,1)}, u32[]{:S(2)}, u32[]{:S(2)}) collective-permute-start(bf16[8,12,128,128]{3,2,1,0:T(8,128)(2,1)S(1)} %all-to-all-done.3.refs_2_.refs_4_), channel_id=1, source_target_pairs={{0,8},{8,0},{16,24},{24,16},{1,9},{9,1},{17,25},{25,17},{2,10},{10... | collective-permute-start | bytes 9437192 | tf_op jit(solution)/shard_map/ppermute | solution.py:277
  366.3 136.6 %collective-permute-start.2 = (bf16[8,12,128,128]{3,2,1,0:T(8,128)(2,1)}, bf16[8,12,128,128]{3,2,1,0:T(8,128)(2,1)}, u32[]{:S(2)}, u32[]{:S(2)}) collective-permute-start(bf16[8,12,128,128]{3,2,1,0:T(8,128)(2,1)} %all-to-all-done.4.refs_3_.refs_5_), channel_id=1, source_target_pairs={{0,8},{8,0},{16,24},{24,16},{1,9},{9,1},{17,25},{25,17},{2,10},{10... | collective-permute-start | bytes 9437192 | tf_op jit(solution)/shard_map/ppermute | solution.py:277
  366.9 140.0 %collective-permute-start.4 = (bf16[8,12,128,128]{3,2,1,0:T(8,128)(2,1)S(1)}, bf16[8,12,128,128]{3,2,1,0:T(8,128)(2,1)}, u32[]{:S(2)}, u32[]{:S(2)}) collective-permute-start(bf16[8,12,128,128]{3,2,1,0:T(8,128)(2,1)S(1)} %all-to-all-done.3.refs_2_.refs_4_), channel_id=1, source_target_pairs={{0,16},{8,24},{16,0},{24,8},{1,17},{9,25},{17,1},{25,9},{2,18},{10... | collective-permute-start | bytes 9437192 | tf_op jit(solution)/shard_map/ppermute | solution.py:277
  368.2 142.9 %collective-permute-start.6 = (bf16[8,12,128,128]{3,2,1,0:T(8,128)(2,1)}, bf16[8,12,128,128]{3,2,1,0:T(8,128)(2,1)}, u32[]{:S(2)}, u32[]{:S(2)}) collective-permute-start(bf16[8,12,128,128]{3,2,1,0:T(8,128)(2,1)} %all-to-all-done.4.refs_3_.refs_5_), channel_id=1, source_target_pairs={{0,16},{8,24},{16,0},{24,8},{1,17},{9,25},{17,1},{25,9},{2,18},{10... | collective-permute-start | bytes 9437192 | tf_op jit(solution)/shard_map/ppermute | solution.py:277
  438.7 124.8 %collective-permute-start.1 = (bf16[4,12,128,128]{3,2,1,0:T(8,128)(2,1)}, bf16[4,12,128,128]{3,2,1,0:T(8,128)(2,1)}, u32[]{:S(2)}, u32[]{:S(2)}) collective-permute-start(bf16[4,12,128,128]{3,2,1,0:T(8,128)(2,1)} %slice.46), channel_id=1, source_target_pairs={{0,16},{8,24},{16,0},{24,8},{1,17},{9,25},{17,1},{25,9},{2,18},{10... | collective-permute-start | bytes 4718600 | tf_op jit(solution)/shard_map/ppermute | solution.py:370
  505.6 66.1 %collective-permute-start.3 = (bf16[4,12,128,128]{3,2,1,0:T(8,128)(2,1)}, bf16[4,12,128,128]{3,2,1,0:T(8,128)(2,1)}, u32[]{:S(2)}, u32[]{:S(2)}) collective-permute-start(bf16[4,12,128,128]{3,2,1,0:T(8,128)(2,1)} %slice.47), channel_id=1, source_target_pairs={{0,16},{8,24},{16,0},{24,8},{1,17},{9,25},{17,1},{25,9},{2,18},{10... | collective-permute-start | bytes 4718600 | tf_op jit(solution)/shard_map/ppermute | solution.py:370
  509.6 62.1 %collective-permute-start.5 = (bf16[4,12,128,128]{3,2,1,0:T(8,128)(2,1)}, bf16[4,12,128,128]{3,2,1,0:T(8,128)(2,1)S(1)}, u32[]{:S(2)}, u32[]{:S(2)}) collective-permute-start(bf16[4,12,128,128]{3,2,1,0:T(8,128)(2,1)} %slice.48), channel_id=1, source_target_pairs={{0,8},{8,0},{16,24},{24,16},{1,9},{9,1},{17,25},{25,17},{2,10},{10... | collective-permute-start | bytes 4718600 | tf_op jit(solution)/shard_map/ppermute | solution.py:371
  513.8 65.4 %collective-permute-start.7 = (bf16[4,12,128,128]{3,2,1,0:T(8,128)(2,1)}, bf16[4,12,128,128]{3,2,1,0:T(8,128)(2,1)S(1)}, u32[]{:S(2)}, u32[]{:S(2)}) collective-permute-start(bf16[4,12,128,128]{3,2,1,0:T(8,128)(2,1)} %slice.49), channel_id=1, source_target_pairs={{0,8},{8,0},{16,24},{24,16},{1,9},{9,1},{17,25},{25,17},{2,10},{10... | collective-permute-start | bytes 4718600 | tf_op jit(solution)/shard_map/ppermute | solution.py:371
  571.8 7.4 %copy-start.5 = (bf16[4,12,128,128]{3,2,1,0:T(8,128)(2,1)}, bf16[4,12,128,128]{3,2,1,0:T(8,128)(2,1)S(1)}, u32[]{:S(2)}) copy-start(bf16[4,12,128,128]{3,2,1,0:T(8,128)(2,1)S(1)} %collective-permute-done.5.refs_4_) | copy-start | bytes 4718596
  579.2 1.1 copy-start.6
  612.8 13.4 %copy-start.12 = (s32[8,32]{1,0:T(8,128)S(1)}, s32[8,32]{1,0:T(8,128)}, u32[]{:S(2)}) copy-start(s32[8,32]{1,0:T(8,128)} %copy-done.11) | copy-start | bytes 3076
Sparse Core Ops, SparseCore 0:
  9.6 153.8 all-gather.12
